TPU v7x, 256 devices: a whole 4x4x8 slice. The times are simulated.
256 devices in a mesh: tm: 32 (over z, y_hi, core), plane: 8 (over x, y_lo).
Axes of the slice: x: 4, y: 4 (y_hi: 2, y_lo: 2; y = y_hi * 2 + y_lo), z: 8, core: 2. Of those that a mesh axis runs over, the one named last changes fastest.
Arguments:
- frames: bfloat16 [64, 8, 512, 1024], P('tm', 'plane'), may hold values from -6 to 6
- template: bfloat16 [32, 8, 128, 128], P('tm', 'plane'), may hold values from -6 to 6
- shift_codes: int32 [64, 2, 32], P('tm'), may hold values from -128 to 127
Outputs:
- correlation: float32 [64, 32, 256], P('tm', 'plane')
- new_template: float32 [32, 8, 128, 128], P('tm', 'plane')
Inputs may be any that keep to these rules, and one draw needn't show every extreme that they name: shift_codes is 16 times the shift in pixels, its integer part at most 8 pixels either way; every plane of a volume shares it.
All inputs are finite; a program needn't handle non-finite values.
Results may differ from a plain program's by a relative error of at most 0.0065.
Values may be sent and summed in bfloat16 or wider, within the bound.
A program may use at most 128 MiB of HBM per device.

v0:
```python
import math

import jax
import jax.numpy as jnp
from jax import lax
from jax.sharding import PartitionSpec as P

SHIFT = 8
WIN = 16
TAPS = 8
SUB = 16


full_turn = 2.0 * math.pi


def dft_tables(block_size):
    positions = jnp.arange(block_size, dtype=jnp.int32)
    product = jnp.mod(positions[:, None] * positions[None, :], block_size)
    angles = product.astype(jnp.float32) * (full_turn / block_size)
    return (jnp.cos(angles).astype(jnp.bfloat16), (-jnp.sin(angles)).astype(jnp.bfloat16))


def spectrum(blocks, cosine_table, sine_table):
    row_real = jnp.einsum(
        "...rc,ck->...rk", blocks, cosine_table, preferred_element_type=jnp.float32
    ).astype(jnp.bfloat16)
    row_imag = jnp.einsum(
        "...rc,ck->...rk", blocks, sine_table, preferred_element_type=jnp.float32
    ).astype(jnp.bfloat16)
    real_part = jnp.einsum(
        "kr,...rl->...kl", cosine_table, row_real, preferred_element_type=jnp.float32
    ) - jnp.einsum("kr,...rl->...kl", sine_table, row_imag, preferred_element_type=jnp.float32)
    imag_part = jnp.einsum(
        "kr,...rl->...kl", cosine_table, row_imag, preferred_element_type=jnp.float32
    ) + jnp.einsum("kr,...rl->...kl", sine_table, row_real, preferred_element_type=jnp.float32)
    return (real_part, imag_part)


def normalized_cross(frame_real, frame_imag, temp_real, temp_imag):
    temp_real = temp_real.astype(jnp.float32)
    temp_imag = temp_imag.astype(jnp.float32)
    cross_real = frame_real * temp_real + frame_imag * temp_imag
    cross_imag = frame_imag * temp_real - frame_real * temp_imag
    magnitude = jnp.sqrt(cross_real * cross_real + cross_imag * cross_imag)
    mean_mag = jnp.mean(magnitude, axis=(-2, -1), keepdims=True) + 1e-06
    return (cross_real / (magnitude + mean_mag), cross_imag / (magnitude + mean_mag))


def window_tables(shifts, block_size, window):
    offsets = jnp.arange(window, dtype=jnp.int32) - window // 2
    lags = jnp.mod(shifts[:, None] + offsets[None, :], block_size)
    positions = jnp.arange(block_size, dtype=jnp.int32)
    product = jnp.mod(positions[None, :, None] * lags[:, None, :], block_size)
    angles = product.astype(jnp.float32) * (full_turn / block_size)
    return (jnp.cos(angles), jnp.sin(angles))


def windows(norm_real, norm_imag, shift_rows, shift_cols, block_size, window):
    highest = lax.Precision.HIGHEST
    row_cos, row_sin = window_tables(shift_rows, block_size, window)
    col_cos, col_sin = window_tables(shift_cols, block_size, window)
    prod_real = jnp.einsum("nkl,nlc->nkc", norm_real, col_cos, precision=highest) - jnp.einsum(
        "nkl,nlc->nkc", norm_imag, col_sin, precision=highest
    )
    prod_imag = jnp.einsum("nkl,nlc->nkc", norm_real, col_sin, precision=highest) + jnp.einsum(
        "nkl,nlc->nkc", norm_imag, col_cos, precision=highest
    )
    result = jnp.einsum("nka,nkc->nac", row_cos, prod_real, precision=highest) - jnp.einsum(
        "nka,nkc->nac", row_sin, prod_imag, precision=highest
    )
    result = result * (1.0 / block_size)
    return result.reshape(result.shape[0], window * window)


def tap_table(fractions, taps, steps):
    offsets = jnp.arange(taps, dtype=jnp.float32) - (taps // 2 - 1)
    spots = offsets - fractions[..., None].astype(jnp.float32) / steps
    raw_taps = jnp.sinc(spots) * jnp.sinc(spots / (taps // 2))
    return raw_taps / jnp.sum(raw_taps, axis=-1, keepdims=True)


def banded(tap_values, offsets, span, block_size, taps):
    inner = jnp.arange(span, dtype=jnp.int32)
    outer = jnp.arange(block_size, dtype=jnp.int32)
    distance = inner[:, None] - outer[None, :] - offsets[..., None, None]
    matrix = jnp.zeros(distance.shape, jnp.float32)
    for tap_index in range(taps):
        matrix = matrix + jnp.where(
            distance == tap_index, tap_values[..., tap_index][..., None, None], 0.0
        )
    return matrix


def on_device(frames, template, shift_codes):
    vol_dev, pl_dev, img_rows, img_cols = frames.shape
    block_size = template.shape[-1]
    across_blocks = img_cols // block_size
    down_blocks = img_rows // block_size
    block_total = across_blocks * down_blocks
    cosine_table, sine_table = dft_tables(block_size)
    part_real, part_imag = spectrum(
        lax.all_gather(template, "tm", axis=0, tiled=True), cosine_table, sine_table
    )
    gathered = jnp.stack([part_real.astype(jnp.bfloat16), part_imag.astype(jnp.bfloat16)], axis=2)
    temp_real = gathered[:, :, 0]
    temp_imag = gathered[:, :, 1]
    blocks = frames.reshape(vol_dev, pl_dev, down_blocks, block_size, across_blocks, block_size)
    blocks = blocks.transpose(0, 2, 4, 1, 3, 5).reshape(
        vol_dev, block_total, pl_dev, block_size, block_size
    )
    frame_real, frame_imag = spectrum(blocks, cosine_table, sine_table)
    norm_real, norm_imag = normalized_cross(frame_real, frame_imag, temp_real, temp_imag)
    shifts = jnp.floor_divide(shift_codes, SUB)
    fractions = jnp.mod(shift_codes, SUB)
    shift_rows = shifts[:, 0, :, None].reshape(-1)
    shift_cols = shifts[:, 1, :, None].reshape(-1)
    local_window = windows(
        norm_real.reshape(-1, block_size, block_size),
        norm_imag.reshape(-1, block_size, block_size),
        shift_rows,
        shift_cols,
        block_size,
        WIN,
    )
    local_window = jnp.sum(local_window.reshape(vol_dev, block_total, pl_dev, WIN * WIN), axis=2)
    correlation = lax.psum_scatter(local_window, "plane", scatter_dimension=1, tiled=True)
    margin = SHIFT + TAPS
    span = block_size + 2 * margin
    tile_count = 1 + (2 * margin + block_size - 1) // block_size
    rows_total = (down_blocks + tile_count - 1) * block_size
    cols_total = (across_blocks + tile_count - 1) * block_size
    padded = jnp.pad(
        frames,
        (
            (0, 0),
            (0, 0),
            (margin, rows_total - img_rows - margin),
            (margin, cols_total - img_cols - margin),
        ),
    )
    tiles = padded.reshape(
        vol_dev,
        pl_dev,
        down_blocks + tile_count - 1,
        block_size,
        across_blocks + tile_count - 1,
        block_size,
    )
    row_join = jnp.concatenate(
        [tiles[:, :, step : step + down_blocks] for step in range(tile_count)], axis=3
    )
    row_join = row_join[:, :, :, :span]
    col_join = jnp.concatenate(
        [row_join[:, :, :, :, step : step + across_blocks] for step in range(tile_count)], axis=5
    )
    col_join = col_join[..., :span]
    regions = col_join.transpose(0, 2, 4, 1, 3, 5).reshape(vol_dev, block_total, pl_dev, span, span)
    highest = lax.Precision.HIGHEST
    part_regions = regions.astype(jnp.float32)
    tap_rows = tap_table(fractions[:, 0], TAPS, SUB)
    tap_cols = tap_table(fractions[:, 1], TAPS, SUB)
    row_offsets = margin + shifts[:, 0] - (TAPS // 2 - 1)
    col_offsets = margin + shifts[:, 1] - (TAPS // 2 - 1)
    row_matrix = banded(tap_rows, row_offsets, span, block_size, TAPS)
    col_matrix = banded(tap_cols, col_offsets, span, block_size, TAPS)
    across = jnp.einsum("vbpqc,vbcj->vbpqj", part_regions, col_matrix, precision=highest)
    summed = lax.psum_scatter(
        jnp.einsum("vbqr,vbpqj->bprj", row_matrix, across, precision=highest),
        "tm",
        scatter_dimension=0,
        tiled=True,
    )
    volumes = vol_dev * lax.axis_size("tm")
    return (correlation, summed * (1.0 / volumes))


def solution(mesh):
    in_specs = (P("tm", "plane", None, None), P("tm", "plane", None, None), P("tm", None, None))
    out_specs = (P("tm", "plane", None), P("tm", "plane", None, None))
    return jax.shard_map(
        on_device, mesh=mesh, in_specs=in_specs, out_specs=out_specs, check_vma=False
    )
```

profile of v0, /device:TPU:8, one launch (start us, length us, event | category | flops | bytes accessed | tf_op | source)
XLA Modules:
  0.0 344.1 jit_solution(1379019673075672570)
XLA Ops:
  7.2 0.7 all-gather.2.cloned.1.call-update
  7.9 2.2 copy.112
  10.2 0.6 copy.59
  10.7 2.3 convolution_convert_fusion
  13.0 1.0 convolution_convert_fusion.1
  14.0 4.1 %copy.111 = bf16[2,1,512,1024]{2,3,0,1:T(8,128)(2,1)} copy(bf16[2,1,512,1024]{3,2,1,0:T(8,128)(2,1)} %param.4) | data formatting | bytes 4194304
  18.2 4.5 %fusion.75 = f32[2,32,128,128]{3,2,1,0:T(8,128)} fusion(bf16[128,2,32,128]{3,0,2,1:T(8,128)(2,1)} %convolution_convert_fusion), kind=kOutput, calls=%fused_computation.106 | convolution fusion | flops 268681216 | bytes 6291456 | tf_op jit(solution)/shard_map/kr,...rl->...kl/dot_general | solution.py:34
  22.6 3.0 fusion.79
  25.9 4.6 %pad.4.clone = bf16[2,1,640,1152]{2,3,0,1:T(8,128)(2,1)} pad(bf16[2,1,512,1024]{2,3,0,1:T(8,128)(2,1)} %copy.111, bf16[]{:T(256)} %constant.133.clone.1), padding=0_0x0_0x16_112x16_112 | pad | bytes 5046274 | tf_op jit(solution)/shard_map/jit(_pad)/pad | solution.py:133
  30.4 7.6 %reshape.254 = bf16[2,1,5,128,9,128]{3,2,5,4,0,1:T(8,128)(2,1)} reshape(bf16[2,1,640,1152]{2,3,0,1:T(8,128)(2,1)} %pad.4.clone) | data formatting | bytes 5898240 | tf_op jit(solution)/shard_map/reshape | solution.py:142
  38.0 6.4 %fusion.266 = (bf16[2,1,4,128,9,128]{3,2,5,4,0,1:T(4,128)(2,1)S(1)}, bf16[2,1,4,128,9,128]{3,2,5,4,0,1:T(4,128)(2,1)S(1)}) fusion(bf16[2,1,5,128,9,128]{3,2,5,4,0,1:T(8,128)(2,1)} %reshape.254), kind=kLoop, calls=%fused_computation.392 | loop fusion | bytes 9437184 | tf_op jit(solution)/shard_map/slice | solution.py:151
  44.4 2.3 fusion.33
  46.7 8.4 %fusion = bf16[2,4,8,1,160,160]{4,1,5,2,0,3:T(4,128)(2,1)} fusion(bf16[2,1,4,160,8,128]{3,2,5,4,0,1:T(4,128)(2,1)S(1)} %fusion.33, bf16[2,1,4,128,9,128]{3,2,5,4,0,1:T(4,128)(2,1)S(1)} %get-tuple-element.18, bf16[2,1,4,128,9,128]{3,2,5,4,0,1:T(4,128)(2,1)S(1)} %get-tuple-element.19), kind=kLoop, calls=%fused_computation.17 | loop fusion | flops 9830400 | bytes 10616832 | tf_op jit(solution)/shard_map/transpose | solution.py:158
  55.1 0.2 fusion.171
  55.4 0.2 broadcast_divide_fusion
  55.6 0.1 add_select_fusion.6
  55.7 12.1 %copy.110 = bf16[2,4,8,1,160,160]{5,4,0,2,1,3:T(8,128)(2,1)} copy(bf16[2,4,8,1,160,160]{4,1,5,2,0,3:T(4,128)(2,1)} %fusion) | data formatting | bytes 6553600 | tf_op jit(solution)/shard_map/reshape.38
  67.9 0.1 copy.80
  68.0 0.1 copy.79
  68.0 0.1 copy.78
  68.1 0.1 copy.77
  68.2 0.1 copy.76
  68.3 0.1 copy.75
  68.4 0.1 copy.74
  68.5 0.1 copy.73
  68.6 0.1 copy.72
  68.7 0.1 copy.90
  68.7 0.1 copy.89
  68.8 0.1 copy.88
  68.9 0.1 copy.87
  69.0 0.1 copy.86
  69.1 0.1 copy.85
  69.2 0.1 copy.84
  69.4 0.1 copy.82
  69.5 5.1 %convolution_add_fusion = f32[2,32,128,128]{3,2,1,0:T(8,128)} fusion(f32[2,32,128,128]{3,2,1,0:T(8,128)} %fusion.75, bf16[128,2,32,128]{3,0,2,1:T(8,128)(2,1)S(1)} %convolution_convert_fusion.1), kind=kOutput, calls=%fused_computation.102 | convolution fusion | flops 269746176 | bytes 10485760 | tf_op jit(solution)/shard_map/kr,...rl->...kl/dot_general | solution.py:36
  74.5 12.5 %fusion.17 = f32[2,32,160,128]{3,2,0,1:T(8,128)} fusion(bf16[2,32,160,160]{3,2,0,1:T(8,128)(2,1)} %bitcast.183, f32[2,32]{0,1:T(8,128)S(1)} %copy.80, f32[2,32]{0,1:T(8,128)S(1)} %copy.79, f32[2,32]{0,1:T(8,128)S(1)} %copy.78, f32[2,32]{0,1:T(8,128)S(1)} %copy.77, f32[2,32]{0,1:T(8,128)S(1)} %copy.76, f32[2,32]{0,1:T(8,128)S(1)} %copy.75, ...), kind=kOutput, calls=%fused_computation.35 | convolution fusion | flops 2548039680 | bytes 8603904 | tf_op jit(solution)/shard_map/vbpqc,vbcj->vbpqj/dot_general | solution.py:167
  87.0 3.5 %all-gather.2.cloned.1.call-done = bf16[32,1,128,128]{3,2,1,0:T(8,128)(2,1)} async-done(((bf16[1,1,128,128]{3,2,1,0:T(8,128)(2,1)}), bf16[32,1,128,128]{3,2,1,0:T(8,128)(2,1)}) %all-gather.2.cloned.1.call-update) | async-done | bytes 1048592 | tf_op jit(solution)/shard_map/all_gather | solution.py:103
  90.5 2.0 fusion.85
  92.5 0.7 fusion.127
  93.2 0.7 fusion.84
  93.9 0.7 fusion.129
  94.6 0.7 convert_bitcast_fusion
  95.3 0.7 convert_bitcast_fusion.1
  96.0 0.2 copy-done
  96.2 1.2 copy-done.1
  97.4 1.2 copy-done.2
  98.6 3.3 fusion.74
  102.0 2.4 add_divide_fusion
  104.4 5.6 %fusion.109 = f32[64,128,16]{1,2,0:T(8,128)S(1)} fusion(f32[64,128,128]{1,2,0:T(8,128)S(1)} %bitcast.177, s32[64,16]{1,0:T(8,128)S(1)} %get-tuple-element.47), kind=kOutput, calls=%fused_computation.152 | convolution fusion | flops 203161600 | bytes 4722688 | tf_op jit(solution)/shard_map/nkl,nlc->nkc/dot_general | solution.py:63
  110.0 5.6 %fusion.111 = f32[64,128,16]{1,2,0:T(8,128)S(1)} fusion(f32[64,128,128]{1,2,0:T(8,128)S(1)} %bitcast.178, s32[64,16]{1,0:T(8,128)S(1)} %get-tuple-element.47), kind=kOutput, calls=%fused_computation.153 | convolution fusion | flops 203161600 | bytes 4722688 | tf_op jit(solution)/shard_map/nkl,nlc->nkc/dot_general | solution.py:66
  115.7 5.8 %convolution_subtract_fusion.1 = f32[64,128,16]{1,2,0:T(8,128)S(1)} fusion(f32[64,128,16]{1,2,0:T(8,128)S(1)} %fusion.109, f32[64,128,128]{1,2,0:T(8,128)S(1)} %bitcast.175, s32[64,16]{1,0:T(8,128)S(1)} %get-tuple-element.47), kind=kOutput, calls=%fused_computation.124 | convolution fusion | flops 203292672 | bytes 5246976 | tf_op jit(solution)/shard_map/nkl,nlc->nkc/dot_general | solution.py:63
  121.5 5.6 %convolution_add_fusion.1 = f32[64,128,16]{1,2,0:T(8,128)S(1)} fusion(f32[64,128,16]{1,2,0:T(8,128)S(1)} %fusion.111, f32[64,128,128]{1,2,0:T(8,128)S(1)} %bitcast.176, s32[64,16]{1,0:T(8,128)S(1)} %get-tuple-element.47), kind=kOutput, calls=%fused_computation.123 | convolution fusion | flops 203292672 | bytes 5246976 | tf_op jit(solution)/shard_map/nkl,nlc->nkc/dot_general | solution.py:66
  127.1 3.6 %fusion.100 = f32[64,16,16]{2,1,0:T(8,128)S(1)} fusion(f32[64,128,16]{1,2,0:T(8,128)S(1)} %convolution_subtract_fusion.1, s32[64,16]{1,0:T(8,128)S(1)} %get-tuple-element.46), kind=kOutput, calls=%fused_computation.144 | convolution fusion | flops 27000832 | bytes 593920 | tf_op jit(solution)/shard_map/nka,nkc->nac/dot_general | solution.py:69
  130.7 3.6 %fusion.88 = f32[64,16,16]{2,1,0:T(8,128)S(1)} fusion(f32[64,16,16]{2,1,0:T(8,128)S(1)} %fusion.100, f32[64,128,16]{1,2,0:T(8,128)S(1)} %convolution_add_fusion.1, s32[64,16]{1,0:T(8,128)S(1)} %get-tuple-element.46), kind=kOutput, calls=%fused_computation.126 | convolution fusion | flops 27033600 | bytes 659456 | tf_op jit(solution)/shard_map/nka,nkc->nac/dot_general | solution.py:69
  134.3 0.2 reshape.269
  134.5 0.7 copy.69
  135.3 17.3 %fusion.81 = f32[32,1,128,128]{2,3,0,1:T(8,128)} fusion(f32[2,32,160,128]{3,2,0,1:T(8,128)} %fusion.17, f32[2,32]{0,1:T(8,128)S(1)} %copy.90, f32[2,32]{0,1:T(8,128)S(1)} %copy.89, f32[2,32]{0,1:T(8,128)S(1)} %copy.88, f32[2,32]{0,1:T(8,128)S(1)} %copy.87, f32[2,32]{0,1:T(8,128)S(1)} %copy.86, f32[2,32]{0,1:T(8,128)S(1)} %copy.85, f32[2,32]{0,1:T(8,128)S(1)} %copy.84, ...), kind=kOutput, calls=%fused_computation.116 | convolution fusion | flops 2044723200 | bytes 7424256 | tf_op jit(solution)/shard_map/vbqr,vbpqj->bprj/dot_general | solution.py:169
  152.6 0.6 dynamic-slice
  153.9 57.2 %all-reduce.4.cloned.1.call-done = f32[2,32,256]{2,0,1:T(2,128)} async-done(((f32[2,32,256]{2,0,1:T(2,128)}), f32[2,32,256]{2,0,1:T(2,128)}) %all-reduce.4.cloned.1.call-update) | async-done | bytes 65552
  211.1 0.7 constant_dynamic-slice_fusion
  211.8 0.6 copy.91
  212.4 123.4 %reduce-scatter.2.cloned.1.call-done = f32[1,1,128,128]{2,3,0,1:T(8,128)} async-done(((f32[32,1,128,128]{2,3,0,1:T(8,128)}), f32[1,1,128,128]{2,3,0,1:T(8,128)}) %reduce-scatter.2.cloned.1.call-update) | async-done | bytes 65552 | tf_op jit(solution)/shard_map/reduce_scatter | solution.py:168
  335.8 0.8 broadcast_multiply_fusion
  336.6 0.7 copy.92
  (25 shorter events, 0.5 us)
Async XLA Ops:
  7.2 83.4 %all-gather.2.cloned.1.call-start = ((), (), s32[]{:S(2)}) async-start(), calls=%async_computation.1 | async-start | bytes 1081344 | tf_op jit(solution)/shard_map/all_gather | solution.py:103
  7.9 203.2 %all-reduce.4.cloned.1.call-start = ((), (), s32[]{:S(2)}) async-start(), calls=%async_computation.3 | async-start | bytes 131072
  22.6 3.0 copy-start.4
  90.5 2.7 copy-start.3
  94.6 1.6 copy-start
  94.6 2.8 copy-start.1
  94.6 4.0 %copy-start.2 = (f32[2,32,128,128]{3,2,1,0:T(8,128)S(1)}, f32[2,32,128,128]{3,2,1,0:T(8,128)}, u32[]{:S(2)}) copy-start(f32[2,32,128,128]{3,2,1,0:T(8,128)} %convolution_add_fusion) | copy-start | bytes 12582916
  135.3 17.4 %copy-start.5 = (u32[256]{0:T(256)S(1)}, u32[256]{0:T(256)}, u32[]{:S(2)}) copy-start(u32[256]{0:T(256)} %constant.152) | copy-start | bytes 3076
  135.3 200.5 %reduce-scatter.2.cloned.1.call-start = ((), (), s32[]{:S(2)}) async-start(), calls=%async_computation.2 | async-start | bytes 2162688 | tf_op jit(solution)/shard_map/reduce_scatter | solution.py:168
Sparse Core Ops, SparseCore 0:
  10.8 79.7 all-gather.1
  135.4 75.6 all-reduce.3
  215.2 120.4 reduce-scatter.1
where the time goes:
time: 348 us; the launch traced here: 344 us
  waiting for transfers between devices  185 us (53%)
  matrix products  84.1 us (24%)
  local copies, waits for them, and re-layouts  45.5 us (13%)
  between operations  14.8 us (4%)
  other arithmetic  14.6 us (4%)
    reduce_scatter x1, waiting for transfers between devices, on_device(): lax.psum_scatter(jnp.einsum('vbqr,vbpqj->bprj', row_matrix, across, preci...  123 us
    unnamed x4, waiting for transfers between devices  57.9 us
    dot_general x1, matrix products, on_device(): jnp.einsum('vbqr,vbpqj->bprj', row_matrix, across, precision=highest)  17.3 us
    dot_general x1, matrix products, on_device(): jnp.einsum('vbpqc,vbcj->vbpqj', part_regions, col_matrix, precision=highest)  12.5 us
    another operation x1, local copies, waits for them, and re-layouts  12.1 us
    unnamed x18, local copies, waits for them, and re-layouts  11.6 us
    transpose x1, other arithmetic, on_device(): col_join.transpose(0, 2, 4, 1, 3, 5)  8.42 us
    reshape x1, local copies, waits for them, and re-layouts, on_device(): padded.reshape(vol_dev, pl_dev, down_blocks + tile_count - 1, block_size,...  7.59 us
  transfers between devices with their start and end apart: 3, of which 3 were waited for; matrix products, arithmetic and copies ran while one was open for 29% of the time, Pallas kernels for 0%

commit v1 on v0

v1 whole, which is shorter than its diff:
```python
import numpy as np
import jax
import jax.numpy as jnp
from jax import lax
from jax.experimental import pallas as pl
from jax.experimental.pallas import tpu as pltpu
from jax.sharding import PartitionSpec as P

B = 128
NB = 32
BX = 8
F32 = jnp.float32
BF = jnp.bfloat16


def tables():
    n = np.arange(B)
    ang = 2 * np.pi * ((n[:, None] * n[None, :]) % B) / B
    cos, sin = np.cos(ang), -np.sin(ang)
    h = B // 2
    dr = np.zeros((2 * B, 2 * B))
    for v in range(2):
        dr[v * B : v * B + B, v * h : v * h + h] = cos[:, :h]
        dr[v * B : v * B + B, B + v * h : B + v * h + h] = sin[:, :h]
        dr[v * B : v * B + B, B + v * h] = cos[:, h]
    dc = np.block([[cos, -sin], [sin, cos]])
    lag = np.arange(32) - 16
    ay = 2 * np.pi * ((lag[:, None] * n[None, :]) % B) / B
    ey = np.block([[np.cos(ay), -np.sin(ay)], [np.sin(ay), np.cos(ay)]])
    ax = 2 * np.pi * ((n[:h, None] * lag[None, :]) % B) / B
    w = np.where(n[:h] == 0, 1.0, 2.0)[:, None] / B
    ex = np.zeros((2 * B, B))
    for v in range(2):
        ex[v * h : v * h + h, v * 32 : v * 32 + 32] = w * np.cos(ax)
        ex[B + v * h : B + v * h + h, v * 32 : v * 32 + 32] = -w * np.sin(ax)
        ex[B + v * h, v * 32 : v * 32 + 32] = np.where(lag % 2 == 0, 1.0, -1.0) / B
    i = np.arange(8) - 3
    t = i[None, :] - np.arange(16)[:, None] / 16
    raw = np.sinc(t) * np.sinc(t / 4)
    tap = raw / raw.sum(-1, keepdims=True)
    tap = np.concatenate([tap, np.zeros((16, 248))], 1)
    nn = np.arange(272)
    extc = tap[:, (nn[:, None] - n[None, :] - 5) % 256]
    nr, q = np.arange(144), np.arange(256)
    extr = tap[:, (q[None, :] - nr[:, None] - 5) % 256]
    extr = np.concatenate([extr[..., :B], extr[..., B:]], 0)
    return [np.asarray(x, np.float32).astype(BF) for x in (dr, dc, ey, ex, extc, extr)]


def dot(a, b):
    return jnp.dot(a, b, preferred_element_type=F32)


def lane(shape):
    return lax.broadcasted_iota(jnp.int32, shape, len(shape) - 1)


def row_stage(x0, x1, dr):
    return dot(jnp.concatenate([x0, x1], axis=1), dr)


def own_spectrum(y, dr, dc):
    r = row_stage(y, y, dr)
    rr, ri = r[:, :B], r[:, B:]
    ln = lane((B, B))
    rr2 = jnp.where(ln == 64, ri, rr)
    ri2 = jnp.where((ln == 64) | (ln == 0), 0.0, ri)
    f = dot(dc, jnp.concatenate([rr2, ri2], axis=0).astype(BF))
    fr, fi = f[:B], f[B:]
    main = jnp.where(ln < 64, fr, fi)
    main = jnp.where(ln == 64, pltpu.roll(fi, 64, 1), main)
    nr = jnp.transpose(fr)[64:72]
    ni = jnp.transpose(fi)[64:72]
    row = lax.broadcasted_iota(jnp.int32, (16, B), 0)
    nyq = jnp.where(row == 0, jnp.concatenate([nr, nr], axis=0),
                    pltpu.roll(jnp.concatenate([ni, ni], axis=0), 1, 0))
    return main.astype(BF), nyq.astype(BF)


def stage_tables(extc_b, extr_b, extc, extr):
    def body(f, _):
        extc[f] = extc_b[f].astype(F32)
        extr[f] = extr_b[f].astype(F32)
        extr[16 + f] = extr_b[16 + f].astype(F32)
        return 0
    lax.fori_loop(0, 16, body, 0)


def block_of(i):
    return (i % 8) * 4 + ((i // 8) % 2) * 2 + i // 16


def warp_block(i, codes, x, extc, extr):
    b = block_of(i)
    by, bx = b // BX, b % BX
    row0 = pl.multiple_of(by * B, B)
    col0 = pl.multiple_of(bx * B, B)
    ln = lane((160, B))
    zero = jnp.zeros((96, B), BF)
    total = None
    for v in range(2):
        cy, cx = codes[v, 0, b], codes[v, 1, b]
        sy, fy = jnp.right_shift(cy, 4), jnp.bitwise_and(cy, 15)
        sx, fx = jnp.right_shift(cx, 4), jnp.bitwise_and(cx, 15)
        acol = extc[fx, pl.ds(8 - sx, 256), :].astype(BF)
        arow = jnp.concatenate([extr[fy, pl.ds(8 + sy, 128), :].astype(BF), extr[16 + fy, pl.ds(8 + sy, 128), :].astype(BF)], axis=1)
        left = x[v, pl.ds(row0, 160), pl.ds(col0, B)]
        main = x[v, pl.ds(row0, 160), pl.ds(col0 + B, B)]
        right = x[v, pl.ds(row0, 160), pl.ds(col0 + 2 * B, B)]
        halo = jnp.where(ln < 64, right, left)
        t = dot(jnp.concatenate([main, halo], axis=1), acol).astype(BF)
        o = dot(arow, jnp.concatenate([t, zero], axis=0))
        total = o if total is None else total + o
    return total


def magnitude(re, im):
    sq = re * re + im * im
    return sq * lax.rsqrt(jnp.maximum(sq, 1e-37))


def front(i, x, dr, dc, r64):
    b = block_of(i)
    by, bx = b // BX, b % BX
    row0 = pl.multiple_of(by * B + 16, 16)
    col0 = pl.multiple_of(bx * B + B, B)
    ln = lane((B, B))
    r = row_stage(x[0, pl.ds(row0, B), pl.ds(col0, B)], x[1, pl.ds(row0, B), pl.ds(col0, B)], dr)
    rr, ri = r[:, :B], r[:, B:]
    half = jnp.bitwise_and(ln, 63)
    r64[...] = jnp.where(half == i, pltpu.roll(ri, i, 1), r64[...])
    ri = jnp.where(half == 0, 0.0, ri)
    return dot(dc, jnp.concatenate([rr.astype(BF), ri.astype(BF)], axis=0))


def cross(fr, fi, gr, gi):
    return fr * gr + fi * gi, fi * gr - fr * gi


def middle(b, f, gbuf, cr, ci, mg, sums):
    ln = lane((B, B))
    g = gbuf[b, 0:B, :].astype(F32)
    gs = pltpu.roll(g, 64, 1)
    gr = jnp.where(ln < 64, g, gs)
    gi = jnp.where(ln < 64, gs, g)
    re, im = cross(f[:B], f[B:], gr, gi)
    m = magnitude(re, im)
    cr[b], ci[b], mg[b] = re, im, m
    sums[pl.ds(b, 1), :] = jnp.sum(m, axis=0, keepdims=True)


def nyquist(gbuf, r64, dc, ey, sums, mean, q64):
    f = dot(dc, jnp.concatenate([r64[...].astype(BF), jnp.zeros((B, B), BF)], axis=0))
    z = jnp.zeros((32, B), F32)
    g = gbuf[:, B : B + 16, :].astype(F32)
    gr, gi = g[:, 0, :], g[:, 1, :]
    gr = jnp.transpose(jnp.concatenate([gr, z, gr, z], axis=0))
    gi = jnp.transpose(jnp.concatenate([gi, z, gi, z], axis=0))
    re, im = cross(f[:B], f[B:], gr, gi)
    m = magnitude(re, im)
    m64 = jnp.sum(m, axis=0, keepdims=True)
    ln = lane((NB, B))
    half = jnp.bitwise_and(ln, 63)
    diag = half == lax.broadcasted_iota(jnp.int32, (NB, B), 0)
    s = sums[...] * jnp.where(half == 0, 1.0, 2.0) + jnp.where(diag, m64, 0.0)
    s0 = jnp.sum(jnp.where(ln < 64, s, 0.0), axis=1, keepdims=True)
    s1 = jnp.sum(jnp.where(ln < 64, 0.0, s), axis=1, keepdims=True)
    mm = jnp.where(ln < 64, s0, s1) * (1.0 / (B * B)) + 1e-6
    mean[...] = mm
    mrow = jnp.sum(jnp.where(diag, mm, 0.0), axis=0, keepdims=True)
    live = jnp.bitwise_and(lane((1, B)), 63) < NB
    inv = 1.0 / (m + jnp.where(live, mrow, 1.0))
    w = jnp.concatenate([(re * inv).astype(BF), (im * inv).astype(BF)], axis=0)
    q64[...] = dot(ey, w)[0:32]


def back(i, codes, cr, ci, mg, mean, q64, ey, ex, win, flat):
    b = block_of(i)
    inv = 1.0 / (mg[i] + mean[pl.ds(i, 1), :])
    w = jnp.concatenate([(cr[i] * inv).astype(BF), (ci[i] * inv).astype(BF)], axis=0)
    q = dot(ey, w)
    half = jnp.bitwise_and(lane((32, B)), 63)
    qi = jnp.where(half == 0, pltpu.roll(q64[...], jnp.bitwise_and(B - i, B - 1), 1), q[32:64])
    c = dot(jnp.concatenate([q[0:32].astype(BF), qi.astype(BF)], axis=1), ex)
    win[i] = c
    for v in range(2):
        sy = jnp.right_shift(codes[v, 0, b], 4)
        sx = jnp.right_shift(codes[v, 1, b], 4)
        piece = win[i, pl.ds(sy + 8, 16), :]
        piece = pltpu.roll(piece, jnp.bitwise_and(B - (8 + 32 * v) - sx, B - 1), 1)
        row = (b // 4) * 8 + v * 4 + b % 4
        flat[pl.ds(row, 16, stride=64), :] = piece


def flatten(flat):
    ln = lane((64, B))
    tiles = []
    for t in range(2):
        out = None
        for k in range(8):
            a = t * 8 + k
            piece = flat[a * 64 : a * 64 + 64, :]
            if k:
                piece = pltpu.roll(piece, 16 * k, 1)
            out = piece if out is None else jnp.where(ln >= 16 * k, piece, out)
        tiles.append(out)
    return tiles


MESH = pl.DeviceIdType.MESH
VM = pl.BlockSpec(memory_space=pltpu.VMEM)
ANY = pl.BlockSpec(memory_space=pl.ANY)
SM = pl.BlockSpec(memory_space=pltpu.SMEM)
UN = 4


def place():
    tm = lax.axis_index("tm")
    return tm // 4, (tm // 2) % 2, tm % 2, lax.axis_index("plane")


def at(z, yh, c, p):
    return (z * 4 + yh * 2 + c, p)


def partners(with_plane):
    z, yh, c, p = place()
    ids = [at((z + d) % 8, yh, c, p) for d in range(1, 8)]
    ids += [at(z, 1 - yh, c, p), at(z, yh, 1 - c, p)]
    if with_plane:
        ids += [at(z, yh, c, (p + d) % 8) for d in range(1, 8)]
    return ids


def greet(with_plane):
    sem = pltpu.get_barrier_semaphore()
    ids = partners(with_plane)
    for dev in ids:
        pl.semaphore_signal(sem, inc=1, device_id=dev, device_id_type=MESH)
    pl.semaphore_wait(sem, len(ids))


def remote(src, dst, send, recv, dev):
    return pltpu.make_async_remote_copy(
        src_ref=src, dst_ref=dst, send_sem=send, recv_sem=recv, device_id=dev, device_id_type=MESH
    )


def gather_kernel(y, dr, dc, out, g, send, recv):
    z, yh, c, p = place()
    mine = c * 16 + yh * 8 + z
    main, nyq = own_spectrum(y[0, 0], dr[...], dc[...])
    g[mine, 0:B, :] = main
    g[mine, B : B + 16, :] = nyq
    greet(False)
    first = []
    for d in range(1, 8):
        cp = remote(g.at[mine], g.at[mine], send.at[d], recv.at[d], at((z + d) % 8, yh, c, p))
        cp.start()
        first.append(cp)
    for cp in first:
        cp.wait()
    own = pl.ds(c * 16 + yh * 8, 8)
    cp = remote(g.at[own], g.at[own], send.at[8], recv.at[8], at(z, 1 - yh, c, p))
    cp.start()
    cp.wait()
    own = pl.ds(c * 16, 16)
    cp = remote(g.at[own], g.at[own], send.at[9], recv.at[9], at(z, yh, 1 - c, p))
    cp.start()
    cp.wait()
    out[...] = g[...]


def zero_pads(x):
    x[:, 0:16, :] = jnp.zeros((2, 16, 1280), BF)
    x[:, 528:544, :] = jnp.zeros((2, 16, 1280), BF)
    x[:, :, 0:B] = jnp.zeros((2, 544, B), BF)
    x[:, :, 1152:1280] = jnp.zeros((2, 544, B), BF)


def compute_kernel(codes, frames, g, dr, dc, ey, ex, extc_b, extr_b, part, corr,
                   x, extc, extr, r64, cr, ci, mg, sums, mean, q64, win, flat, sem):
    cp = pltpu.make_async_copy(frames.at[:, 0], x.at[:, 16:528, B:1152], sem)
    cp.start()
    zero_pads(x)
    stage_tables(extc_b, extr_b, extc, extr)
    r64[...] = jnp.zeros_like(r64)
    cp.wait()

    def warp_step(i, _):
        part[i] = warp_block(i, codes, x, extc, extr).astype(BF)
        return 0

    def front_step(i, _):
        f = front(i, x, dr[...], dc[...], r64)
        middle(i, f, g, cr, ci, mg, sums)
        return 0

    def back_step(i, _):
        back(i, codes, cr, ci, mg, mean, q64, ey[...], ex[...], win, flat)
        return 0

    lax.fori_loop(0, NB, warp_step, 0, unroll=UN)
    lax.fori_loop(0, NB, front_step, 0, unroll=UN)
    nyquist(g, r64, dc[...], ey[...], sums, mean, q64)
    lax.fori_loop(0, NB, back_step, 0, unroll=UN)
    t = flatten(flat)
    corr[:, 0:B] = t[0]
    corr[:, B : 2 * B] = t[1]


def reduce_kernel(part, corr, out_c, out_t, ra, sb, rb, sc, rc, rp, send, recv):
    z, yh, c, p = place()
    greet(True)
    far = []
    for d in range(1, 8):
        q = (p + d) % 8
        cp = remote(corr.at[pl.ds(pl.multiple_of(q * 8, 8), 8)], rp.at[d - 1], send.at[d], recv.at[d], at(z, yh, c, q))
        cp.start()
        far.append(cp)
    cp = remote(part.at[pl.ds((1 - c) * 16, 16)], ra, send.at[8], recv.at[8], at(z, yh, 1 - c, p))
    cp.start()
    cp.wait()

    def add_a(j, _):
        sb[j] = (part[c * 16 + j].astype(F32) + ra[j].astype(F32)).astype(BF)
        return 0

    lax.fori_loop(0, 16, add_a, 0)
    cp = remote(sb.at[pl.ds((1 - yh) * 8, 8)], rb, send.at[9], recv.at[9], at(z, 1 - yh, c, p))
    cp.start()
    cp.wait()

    def add_b(j, _):
        sc[j] = (sb[yh * 8 + j].astype(F32) + rb[j].astype(F32)).astype(BF)
        return 0

    lax.fori_loop(0, 8, add_b, 0)
    near = []
    for d in range(1, 8):
        q = (z + d) % 8
        cp = remote(sc.at[q], rc.at[d - 1], send.at[9 + d], recv.at[9 + d], at(q, yh, c, p))
        cp.start()
        near.append(cp)
    for cp in far:
        cp.wait()
    total = corr[pl.ds(pl.multiple_of(p * 8, 8), 8), :]
    for d in range(7):
        total = total + rp[d]
    out_c[...] = total
    for cp in near:
        cp.wait()
    total = sc[z].astype(F32)
    for d in range(7):
        total = total + rc[d].astype(F32)
    out_t[...] = total * (1.0 / 64)


def on_device(frames, template, codes):
    dr, dc, ey, ex, extc, extr = tables()
    big = pltpu.CompilerParams(vmem_limit_bytes=60 * 2**20)
    dma = pltpu.SemaphoreType.DMA
    g = pl.pallas_call(
        gather_kernel,
        out_shape=jax.ShapeDtypeStruct((NB, 144, B), BF),
        in_specs=[VM] * 3, out_specs=VM,
        scratch_shapes=[pltpu.VMEM((NB, 144, B), BF), dma((10,)), dma((10,))],
        compiler_params=pltpu.CompilerParams(collective_id=0, has_side_effects=True),
    )(template, dr, dc)
    part, corr = pl.pallas_call(
        compute_kernel,
        out_shape=[jax.ShapeDtypeStruct((NB, B, B), BF), jax.ShapeDtypeStruct((64, 256), F32)],
        in_specs=[SM, ANY] + [VM] * 7, out_specs=[VM, VM],
        scratch_shapes=[
            pltpu.VMEM((2, 544, 1280), BF), pltpu.VMEM((16, 272, B), F32), pltpu.VMEM((32, 144, B), F32),
            pltpu.VMEM((B, B), F32), pltpu.VMEM((NB, B, B), F32), pltpu.VMEM((NB, B, B), F32), pltpu.VMEM((NB, B, B), F32),
            pltpu.VMEM((NB, B), F32), pltpu.VMEM((NB, B), F32), pltpu.VMEM((32, B), F32),
            pltpu.VMEM((NB, 32, B), F32), pltpu.VMEM((1024, B), F32), dma,
        ],
        compiler_params=big,
    )(codes, frames, g, dr, dc, ey, ex, extc, extr)
    out_c, out_t = pl.pallas_call(
        reduce_kernel,
        out_shape=[jax.ShapeDtypeStruct((8, 256), F32), jax.ShapeDtypeStruct((B, B), F32)],
        in_specs=[VM, VM], out_specs=[VM, VM],
        scratch_shapes=[
            pltpu.VMEM((16, B, B), BF), pltpu.VMEM((16, B, B), BF), pltpu.VMEM((8, B, B), BF), pltpu.VMEM((8, B, B), BF),
            pltpu.VMEM((7, B, B), BF), pltpu.VMEM((7, 8, 256), F32), dma((17,)), dma((17,)),
        ],
        compiler_params=pltpu.CompilerParams(collective_id=1, has_side_effects=True, vmem_limit_bytes=32 * 2**20),
    )(part, corr)
    return out_c.reshape(2, 4, 256), out_t.reshape(1, 1, B, B)


def solution(mesh):
    in_specs = (P("tm", "plane", None, None), P("tm", "plane", None, None), P("tm", None, None))
    out_specs = (P("tm", "plane", None), P("tm", "plane", None, None))
    return jax.shard_map(on_device, mesh=mesh, in_specs=in_specs, out_specs=out_specs, check_vma=False)
```

time: 348 us -> 76.1 us (0.22)
  the two profiles are of different devices: /device:TPU:8 before, /device:TPU:24 now
where the time goes in v1:
time: 76.1 us; the launch traced here: 75.8 us
  Pallas kernels  71.9 us (94%)
  local copies, waits for them, and re-layouts  3.29 us (4%)
    pallas_call x1, Pallas kernels, on_device(): pl.pallas_call(gather_kernel, out_shape=jax.ShapeDtypeStruct((NB, 144, B)...  27.1 us
    pallas_call x1, Pallas kernels, on_device(): pl.pallas_call(reduce_kernel, out_shape=[jax.ShapeDtypeStruct((8, 256), F...  24.2 us
    pallas_call x1, Pallas kernels, on_device(): pl.pallas_call(compute_kernel, out_shape=[jax.ShapeDtypeStruct((NB, B, B)...  20.6 us
    unnamed x5, local copies, waits for them, and re-layouts  2.69 us

profile of v1, /device:TPU:24, one launch (start us, length us, event | category | flops | bytes accessed | tf_op | source)
XLA Modules:
  0.0 75.8 jit_solution(15053135800641428075)
XLA Ops:
  0.6 27.1 %shard_map.104.g = bf16[32,144,128]{2,1,0:T(8,128)(2,1)} custom-call(bf16[1,1,128,128]{3,2,1,0:T(8,128)(2,1)} %y.1, bf16[256,256]{1,0:T(8,128)(2,1)} %constant.12.clone.dr, bf16[256,256]{1,0:T(8,128)(2,1)} %constant.13.clone.dc), custom_call_target="tpu_custom_call" | custom-call | tf_op jit(solution)/shard_map/pallas_call | solution.py:363
  27.7 20.6 %shard_map.105 = (bf16[32,128,128]{2,1,0:T(8,128)(2,1)}, f32[64,256]{1,0:T(8,128)}) custom-call(s32[2,2,32]{2,1,0:T(2,128)} %codes.1, bf16[2,1,512,1024]{3,2,1,0:T(8,128)(2,1)} %frames.1, bf16[32,144,128]{2,1,0:T(8,128)(2,1)} %shard_map.104.g, bf16[256,256]{1,0:T(8,128)(2,1)} %constant.12.clone.dr, bf16[256,256]{1,0:T(8,128)(2,1)} %constant.13.clone.dc, ...), custom_call_target="tpu_custom_call" | custom-call | tf_op jit(solution)/shard_map/pallas_call | solution.py:370
  48.3 0.0 copy-start
  48.3 1.2 %copy-done = bf16[32,128,128]{2,1,0:T(8,128)(2,1)S(1)} copy-done((bf16[32,128,128]{2,1,0:T(8,128)(2,1)S(1)}, bf16[32,128,128]{2,1,0:T(8,128)(2,1)}, u32[]{:S(2)}) %copy-start) | copy-done | bytes 1048600
  49.5 0.0 copy-start.1
  49.5 0.8 %copy-done.1 = f32[64,256]{1,0:T(8,128)S(1)} copy-done((f32[64,256]{1,0:T(8,128)S(1)}, f32[64,256]{1,0:T(8,128)}, u32[]{:S(2)}) %copy-start.1) | copy-done | bytes 65560
  50.4 24.2 %shard_map.106 = (f32[8,256]{1,0:T(8,128)S(1)}, f32[128,128]{1,0:T(8,128)S(1)}) custom-call(bf16[32,128,128]{2,1,0:T(8,128)(2,1)S(1)} %copy-done, f32[64,256]{1,0:T(8,128)S(1)} %copy-done.1), custom_call_target="tpu_custom_call" | custom-call | tf_op jit(solution)/shard_map/pallas_call | solution.py:382
  74.6 0.6 reshape.10
  75.2 0.6 copy.12
Async XLA Ops:
  48.3 1.2 %copy-start = (bf16[32,128,128]{2,1,0:T(8,128)(2,1)S(1)}, bf16[32,128,128]{2,1,0:T(8,128)(2,1)}, u32[]{:S(2)}) copy-start(bf16[32,128,128]{2,1,0:T(8,128)(2,1)} %get-tuple-element.6.part) | copy-start | bytes 3145732
  49.5 0.8 %copy-start.1 = (f32[64,256]{1,0:T(8,128)S(1)}, f32[64,256]{1,0:T(8,128)}, u32[]{:S(2)}) copy-start(f32[64,256]{1,0:T(8,128)} %get-tuple-element.7.corr) | copy-start | bytes 196612

commit v2 on v1

v2 whole, which is shorter than its diff:
```python
import numpy as np
import jax
import jax.numpy as jnp
from jax import lax
from jax.experimental import pallas as pl
from jax.experimental.pallas import tpu as pltpu
from jax.sharding import PartitionSpec as P

B = 128
NB = 32
BX = 8
F32 = jnp.float32
BF = jnp.bfloat16


def tables():
    n = np.arange(B)
    ang = 2 * np.pi * ((n[:, None] * n[None, :]) % B) / B
    cos, sin = np.cos(ang), -np.sin(ang)
    h = B // 2
    dr = np.zeros((2 * B, 2 * B))
    for v in range(2):
        dr[v * B : v * B + B, v * h : v * h + h] = cos[:, :h]
        dr[v * B : v * B + B, B + v * h : B + v * h + h] = sin[:, :h]
        dr[v * B : v * B + B, B + v * h] = cos[:, h]
    dc = np.block([[cos, -sin], [sin, cos]])
    lag = np.arange(32) - 16
    ay = 2 * np.pi * ((lag[:, None] * n[None, :]) % B) / B
    ey = np.block([[np.cos(ay), -np.sin(ay)], [np.sin(ay), np.cos(ay)]])
    ax = 2 * np.pi * ((n[:h, None] * lag[None, :]) % B) / B
    w = np.where(n[:h] == 0, 1.0, 2.0)[:, None] / B
    ex = np.zeros((2 * B, B))
    for v in range(2):
        ex[v * h : v * h + h, v * 32 : v * 32 + 32] = w * np.cos(ax)
        ex[B + v * h : B + v * h + h, v * 32 : v * 32 + 32] = -w * np.sin(ax)
        ex[B + v * h, v * 32 : v * 32 + 32] = np.where(lag % 2 == 0, 1.0, -1.0) / B
    i = np.arange(8) - 3
    t = i[None, :] - np.arange(16)[:, None] / 16
    raw = np.sinc(t) * np.sinc(t / 4)
    tap = raw / raw.sum(-1, keepdims=True)
    tap = np.concatenate([tap, np.zeros((16, 248))], 1)
    nn = np.arange(272)
    extc = tap[:, (nn[:, None] - n[None, :] - 5) % 256]
    nr, q = np.arange(144), np.arange(256)
    extr = tap[:, (q[None, :] - nr[:, None] - 5) % 256]
    ext = np.concatenate([extc[:, :144], extc[:, 256:272], extr[..., :B], extr[:, 112:144, B:]], 1)
    return [np.asarray(x, np.float32).astype(BF) for x in (dr, dc, ey, ex, ext)]


def dot(a, b):
    return jnp.dot(a, b, preferred_element_type=F32)


def lane(shape):
    return lax.broadcasted_iota(jnp.int32, shape, len(shape) - 1)


def row_stage(x0, x1, dr):
    return dot(jnp.concatenate([x0, x1], axis=1), dr)


def own_spectrum(y, dr, dc):
    r = row_stage(y, y, dr)
    rr, ri = r[:, :B], r[:, B:]
    ln = lane((B, B))
    rr2 = jnp.where(ln == 64, ri, rr)
    ri2 = jnp.where((ln == 64) | (ln == 0), 0.0, ri)
    f = dot(dc, jnp.concatenate([rr2, ri2], axis=0).astype(BF))
    fr, fi = f[:B], f[B:]
    main = jnp.where(ln < 64, fr, fi)
    main = jnp.where(ln == 64, pltpu.roll(fi, 64, 1), main)
    nr = jnp.transpose(fr)[64:72]
    ni = jnp.transpose(fi)[64:72]
    row = lax.broadcasted_iota(jnp.int32, (16, B), 0)
    nyq = jnp.where(row == 0, jnp.concatenate([nr, nr], axis=0),
                    pltpu.roll(jnp.concatenate([ni, ni], axis=0), 1, 0))
    return main.astype(BF), nyq.astype(BF)


def stage_tables(ext, extc, extr):
    zero = jnp.zeros((112, B), F32)

    def body(f, _):
        extc[f, 0:144] = ext[f, 0:144].astype(F32)
        extc[f, 144:256] = zero
        extc[f, 256:272] = ext[f, 144:160].astype(F32)
        extr[f] = ext[f, 160:304].astype(F32)
        extr[16 + f, 0:112] = zero
        extr[16 + f, 112:144] = ext[f, 304:336].astype(F32)
        return 0

    lax.fori_loop(0, 16, body, 0)


def block_of(i):
    return (i % 8) * 4 + ((i // 8) % 2) * 2 + i // 16


def warp_block(i, codes, x, extc, extr):
    b = block_of(i)
    by, bx = b // BX, b % BX
    row0 = pl.multiple_of(by * B, B)
    col0 = pl.multiple_of(bx * B, B)
    ln = lane((160, B))
    zero = jnp.zeros((96, B), BF)
    total = None
    for v in range(2):
        cy, cx = codes[v, 0, b], codes[v, 1, b]
        sy, fy = jnp.right_shift(cy, 4), jnp.bitwise_and(cy, 15)
        sx, fx = jnp.right_shift(cx, 4), jnp.bitwise_and(cx, 15)
        acol = extc[fx, pl.ds(8 - sx, 256), :].astype(BF)
        arow = jnp.concatenate([extr[fy, pl.ds(8 + sy, 128), :].astype(BF), extr[16 + fy, pl.ds(8 + sy, 128), :].astype(BF)], axis=1)
        left = x[v, pl.ds(row0, 160), pl.ds(col0, B)]
        main = x[v, pl.ds(row0, 160), pl.ds(col0 + B, B)]
        right = x[v, pl.ds(row0, 160), pl.ds(col0 + 2 * B, B)]
        halo = jnp.where(ln < 64, right, left)
        t = dot(jnp.concatenate([main, halo], axis=1), acol).astype(BF)
        o = dot(arow, jnp.concatenate([t, zero], axis=0))
        total = o if total is None else total + o
    return total


def magnitude(re, im):
    sq = re * re + im * im
    return sq * lax.rsqrt(jnp.maximum(sq, 1e-37))


def front(i, x, dr, dc, r64, cr, ci):
    b = block_of(i)
    by, bx = b // BX, b % BX
    row0 = pl.multiple_of(by * B + 16, 16)
    col0 = pl.multiple_of(bx * B + B, B)
    ln = lane((B, B))
    r = row_stage(x[0, pl.ds(row0, B), pl.ds(col0, B)], x[1, pl.ds(row0, B), pl.ds(col0, B)], dr)
    rr, ri = r[:, :B], r[:, B:]
    half = jnp.bitwise_and(ln, 63)
    r64[...] = jnp.where(half == i, pltpu.roll(ri, i, 1), r64[...])
    ri = jnp.where(half == 0, 0.0, ri)
    f = dot(dc, jnp.concatenate([rr.astype(BF), ri.astype(BF)], axis=0))
    cr[i] = f[:B]
    ci[i] = f[B:]


def cross(fr, fi, gr, gi):
    return fr * gr + fi * gi, fi * gr - fr * gi


def middle(b, gbuf, cr, ci, mg, sums):
    ln = lane((B, B))
    g = gbuf[b, 0:B, :].astype(F32)
    gs = pltpu.roll(g, 64, 1)
    gr = jnp.where(ln < 64, g, gs)
    gi = jnp.where(ln < 64, gs, g)
    re, im = cross(cr[b], ci[b], gr, gi)
    m = magnitude(re, im)
    cr[b], ci[b], mg[b] = re, im, m
    sums[pl.ds(b, 1), :] = jnp.sum(m, axis=0, keepdims=True)


def nyquist(gbuf, r64, dc, ey, sums, mean, q64):
    f = dot(dc, jnp.concatenate([r64[...].astype(BF), jnp.zeros((B, B), BF)], axis=0))
    z = jnp.zeros((32, B), F32)
    g = gbuf[:, B : B + 16, :].astype(F32)
    gr, gi = g[:, 0, :], g[:, 1, :]
    gr = jnp.transpose(jnp.concatenate([gr, z, gr, z], axis=0))
    gi = jnp.transpose(jnp.concatenate([gi, z, gi, z], axis=0))
    re, im = cross(f[:B], f[B:], gr, gi)
    m = magnitude(re, im)
    m64 = jnp.sum(m, axis=0, keepdims=True)
    ln = lane((NB, B))
    half = jnp.bitwise_and(ln, 63)
    diag = half == lax.broadcasted_iota(jnp.int32, (NB, B), 0)
    s = sums[...] * jnp.where(half == 0, 1.0, 2.0) + jnp.where(diag, m64, 0.0)
    s0 = jnp.sum(jnp.where(ln < 64, s, 0.0), axis=1, keepdims=True)
    s1 = jnp.sum(jnp.where(ln < 64, 0.0, s), axis=1, keepdims=True)
    mm = jnp.where(ln < 64, s0, s1) * (1.0 / (B * B)) + 1e-6
    mean[...] = mm
    mrow = jnp.sum(jnp.where(diag, mm, 0.0), axis=0, keepdims=True)
    live = jnp.bitwise_and(lane((1, B)), 63) < NB
    inv = 1.0 / (m + jnp.where(live, mrow, 1.0))
    w = jnp.concatenate([(re * inv).astype(BF), (im * inv).astype(BF)], axis=0)
    q64[...] = dot(ey, w)[0:32]


def back(k, zt, codes, cr, ci, mg, mean, q64, ey, ex, win, flat):
    i = k * 8 + zt
    b = block_of(i)
    inv = 1.0 / (mg[i] + mean[pl.ds(i, 1), :])
    w = jnp.concatenate([(cr[i] * inv).astype(BF), (ci[i] * inv).astype(BF)], axis=0)
    q = dot(ey, w)
    half = jnp.bitwise_and(lane((32, B)), 63)
    qi = jnp.where(half == 0, pltpu.roll(q64[...], jnp.bitwise_and(B - i, B - 1), 1), q[32:64])
    win[k] = dot(jnp.concatenate([q[0:32].astype(BF), qi.astype(BF)], axis=1), ex)
    for v in range(2):
        sy = jnp.right_shift(codes[v, 0, b], 4)
        sx = jnp.right_shift(codes[v, 1, b], 4)
        piece = win[k, pl.ds(sy + 8, 16), :]
        piece = pltpu.roll(piece, jnp.bitwise_and(B - (8 + 32 * v) - sx, B - 1), 1)
        row = v * 4 + (k % 2) * 2 + k // 2
        flat[pl.ds(row, 16, stride=8), :] = piece


def flatten(flat):
    ln = lane((8, B))
    tiles = []
    for t in range(2):
        out = None
        for k in range(8):
            a = t * 8 + k
            piece = flat[a * 8 : a * 8 + 8, :]
            if k:
                piece = pltpu.roll(piece, 16 * k, 1)
            out = piece if out is None else jnp.where(ln >= 16 * k, piece, out)
        tiles.append(out)
    return jnp.concatenate(tiles, axis=1)


MESH = pl.DeviceIdType.MESH
ANY = pl.BlockSpec(memory_space=pl.ANY)
VM = pl.BlockSpec(memory_space=pltpu.VMEM)
SM = pl.BlockSpec(memory_space=pltpu.SMEM)
NEAR = (1, 7, 2, 6, 3, 5, 4)
FAR = (4, 3, 5, 2, 6, 1, 7, 0)
GZ, GY, GS, SA, SY, SZ, CP, NSEM = 0, 8, 16, 32, 34, 42, 50, 58


def kernel(codes, frames, y_h, dr_h, dc_h, ey_h, ex_h, ext_h, out_c, out_t,
           x, ext, extc, extr, y, dr, dc, ey, ex, g, r64, cr, ci, mg, sums, mean, q64, win, flat, sent,
           part, ra, sb, rb, sc, rc, rp, own, local, send, recv):
    tm = lax.axis_index("tm")
    z, yh, c, p = tm // 4, (tm // 2) % 2, tm % 2, lax.axis_index("plane")

    def at(zz, yy, cc, pp):
        return (zz * 4 + yy * 2 + cc, pp)

    up = [at((z + d) % 8, yh, c, p) for d in range(8)]
    across, sibling = at(z, 1 - yh, c, p), at(z, yh, 1 - c, p)
    peers = [at(z, yh, c, (p + d) % 8) for d in range(8)]

    def slot(cc, yy, zz):
        return cc * 16 + yy * 8 + zz

    def copy(src, dst, sem, dev):
        return pltpu.make_async_remote_copy(
            src_ref=src, dst_ref=dst, send_sem=send.at[sem], recv_sem=recv.at[sem],
            device_id=dev, device_id_type=MESH)

    def spectrum_copy(at_slot, sem, dev):
        return copy(g.at[at_slot], g.at[at_slot], sem, dev)

    barrier = pltpu.get_barrier_semaphore()
    greeted = up[1:] + [across, sibling] + peers[1:]
    for dev in greeted:
        pl.semaphore_signal(barrier, inc=1, device_id=dev, device_id_type=MESH)
    loads = [pltpu.make_async_copy(a, b, local.at[n]) for n, (a, b) in enumerate(
        ((y_h.at[0, 0], y), (dr_h, dr), (dc_h, dc), (ext_h, ext),
         (frames.at[:, 0], x.at[:, 16:528, B:1152]), (ey_h, ey), (ex_h, ex)))]
    for cp in loads:
        cp.start()
    x[:, 0:16, :] = jnp.zeros((2, 16, 1280), BF)
    x[:, 528:544, :] = jnp.zeros((2, 16, 1280), BF)
    x[:, 16:528, 0:B] = jnp.zeros((2, 512, B), BF)
    x[:, 16:528, 1152:1280] = jnp.zeros((2, 512, B), BF)
    r64[...] = jnp.zeros_like(r64)
    for cp in loads[:3]:
        cp.wait()
    mine = slot(c, yh, z)
    main, nyq = own_spectrum(y[...], dr[...], dc[...])
    g[mine, 0:B, :] = main
    g[mine, B : B + 16, :] = nyq
    loads[3].wait()
    stage_tables(ext, extc, extr)
    pl.semaphore_wait(barrier, len(greeted))
    for d in NEAR:
        spectrum_copy(mine, GZ + d, up[d]).start()
    spectrum_copy(mine, GY, across).start()
    spectrum_copy(mine, GS, sibling).start()
    for cp in loads[4:]:
        cp.wait()

    def z_arrived(d):
        s = slot(c, yh, (z + 8 - d) % 8)
        spectrum_copy(s, GZ + d, up[d]).wait_recv()
        spectrum_copy(s, GY + d, across).start()
        spectrum_copy(s, GS + d, sibling).start()

    def y_arrived(d):
        s = slot(c, 1 - yh, (z + 8 - d) % 8)
        spectrum_copy(s, GY + d, across).wait_recv()
        spectrum_copy(s, GS + 8 + d, sibling).start()

    def sibling_arrived(k):
        for d in range(8):
            s = slot(1 - c, yh if k == 0 else 1 - yh, (z + 8 - d) % 8)
            spectrum_copy(s, GS + 8 * k + d, sibling).wait_recv()

    def sum_a(n):
        return copy(part.at[pl.ds(8 * n, 8)], ra.at[pl.ds(8 * n, 8)], SA + n, sibling)

    def sum_y(d):
        t = (z + d) % 8
        return copy(sb.at[t], rb.at[t], SY + d, across)

    def sum_z(d):
        return copy(sc.at[(z + d) % 8], rc.at[d - 1], SZ + d, up[d])

    def both(w):
        return part[16 + w].astype(F32) + ra[w].astype(F32)

    def send_y():
        sum_a(0).wait_recv()
        for d in FAR:
            t = (z + d) % 8
            sb[t] = both(t).astype(BF)
        for d in FAR:
            sum_y(d).start()

    def send_z(ds):
        for d in ds:
            sum_y(d).wait_recv()
            t = (z + d) % 8
            total = both(8 + t) + rb[t].astype(F32)
            if d == 0:
                own[...] = total
            else:
                sc[t] = total.astype(BF)
                sum_z(d).start()

    def slot_of(w):
        cc = jnp.where(w < 16, 1 - c, c)
        yy = jnp.where((w // 8) % 2 == 0, 1 - yh, yh)
        return cc * 16 + yy * 8 + w % 8

    def phase(step, events, order):
        def quarter(n, _):
            q = n if order else 3 - n

            def one(j, _):
                step(q * 8 + j)
                return 0

            lax.fori_loop(0, 8, one, 0, unroll=UN)
            for k, event in events.items():
                pl.when(n == k)(event)
            return 0

        lax.fori_loop(0, 4, quarter, 0)

    def warp_step(w):
        part[w] = warp_block(slot_of(w), codes, x, extc, extr).astype(BF)

    def after_1():
        sum_a(1).start()
        z_arrived(1)
        z_arrived(7)

    def after_2():
        send_y()
        z_arrived(2)
        z_arrived(6)

    def after_3():
        z_arrived(3)
        z_arrived(5)

    phase(warp_step, {0: lambda: sum_a(0).start(), 1: after_1, 2: after_2, 3: after_3}, True)

    def front_step(w):
        front(slot_of(w), x, dr[...], dc[...], r64, cr, ci)

    def front_0():
        z_arrived(4)
        y_arrived(0)

    def arrivals(*ds):
        def event():
            for d in ds:
                y_arrived(d)
        return event

    phase(front_step, {0: front_0, 1: arrivals(1, 7), 2: arrivals(2, 6), 3: arrivals(3, 5, 4)}, True)

    def middle_step(w):
        middle(slot_of(w), g, cr, ci, mg, sums)

    def middle_0():
        sum_a(1).wait_recv()
        send_z(FAR[:4])

    def middle_1():
        send_z(FAR[4:])
        sibling_arrived(0)

    phase(middle_step, {0: middle_0, 1: middle_1, 2: lambda: sibling_arrived(1)}, False)
    nyquist(g, r64, dc[...], ey[...], sums, mean, q64)

    def window_copy(d):
        return copy(sent.at[d], rp.at[d - 1], CP + d, peers[d])

    def back_step(n, _):
        zt = (p + 1 + n) % 8
        for k in range(4):
            back(k, zt, codes, cr, ci, mg, mean, q64, ey[...], ex[...], win, flat)
        sent[(n + 1) % 8] = flatten(flat)
        for d in range(1, 8):
            pl.when(n == d - 1)(lambda d=d: window_copy(d).start())
        return 0

    lax.fori_loop(0, 8, back_step, 0)
    for d in range(1, 8):
        sum_z(d).wait_recv()
    total = own[...]
    for d in range(7):
        total = total + rc[d].astype(F32)
    out_t[0, 0] = total * (1.0 / 64)
    for d in range(1, 8):
        window_copy(d).wait_recv()
    total = sent[0]
    for d in range(7):
        total = total + rp[d]
    out_c[0] = total[0:4]
    out_c[1] = total[4:8]
    for d in range(1, 8):
        spectrum_copy(mine, GZ + d, up[d]).wait_send()
        sum_z(d).wait_send()
        window_copy(d).wait_send()
    for d in range(8):
        spectrum_copy(mine, GY + d, across).wait_send()
        spectrum_copy(mine, GS + d, sibling).wait_send()
        spectrum_copy(mine, GS + 8 + d, sibling).wait_send()
        sum_y(d).wait_send()
    sum_a(0).wait_send()
    sum_a(1).wait_send()


UN = 4


def on_device(frames, template, codes):
    vm = pltpu.VMEM
    dma = pltpu.SemaphoreType.DMA
    return pl.pallas_call(
        kernel,
        out_shape=[jax.ShapeDtypeStruct((2, 4, 256), F32), jax.ShapeDtypeStruct((1, 1, B, B), F32)],
        in_specs=[SM] + [ANY] * 7,
        out_specs=[VM, VM],
        scratch_shapes=[
            vm((2, 544, 1280), BF), vm((16, 336, B), BF), vm((16, 272, B), F32), vm((32, 144, B), F32),
            vm((B, B), BF), vm((2 * B, 2 * B), BF), vm((2 * B, 2 * B), BF), vm((64, 2 * B), BF), vm((2 * B, B), BF),
            vm((NB, 144, B), BF), vm((B, B), F32),
            vm((NB, B, B), F32), vm((NB, B, B), F32), vm((NB, B, B), F32),
            vm((NB, B), F32), vm((NB, B), F32), vm((32, B), F32),
            vm((4, 32, B), F32), vm((B, B), F32), vm((8, 8, 2 * B), F32),
            vm((NB, B, B), BF), vm((16, B, B), BF), vm((8, B, B), BF), vm((8, B, B), BF),
            vm((8, B, B), BF), vm((7, B, B), BF), vm((7, 8, 2 * B), F32), vm((B, B), F32),
            dma((7,)), dma((NSEM,)), dma((NSEM,)),
        ],
        compiler_params=pltpu.CompilerParams(
            collective_id=0, has_side_effects=True, vmem_limit_bytes=48 * 2**20),
    )(codes, frames, template, *tables())


def solution(mesh):
    in_specs = (P("tm", "plane", None, None), P("tm", "plane", None, None), P("tm", None, None))
    out_specs = (P("tm", "plane", None), P("tm", "plane", None, None))
    return jax.shard_map(on_device, mesh=mesh, in_specs=in_specs, out_specs=out_specs, check_vma=False)
```

time: 76.1 us -> 48.1 us (0.63)
  the two profiles are of different devices: /device:TPU:24 before, /device:TPU:8 now
where the time goes in v2:
time: 48.1 us; the launch traced here: 47.7 us
  Pallas kernels  38.1 us (79%)
  local copies, waits for them, and re-layouts  8.99 us (19%)
  between operations  0.65 us (1%)
    pallas_call x1, Pallas kernels, on_device(): pl.pallas_call(kernel, out_shape=[jax.ShapeDtypeStruct((2, 4, 256), F32),...  38.1 us
    unnamed x18, local copies, waits for them, and re-layouts  8.99 us

profile of v2, /device:TPU:8, one launch (start us, length us, event | category | flops | bytes accessed | tf_op | source)
XLA Modules:
  0.0 47.7 jit_solution(893105685723935466)
XLA Ops:
  0.6 0.0 copy-start
  0.6 1.6 %copy-done = bf16[2,1,512,1024]{3,2,1,0:T(8,128)(2,1)S(1)} copy-done((bf16[2,1,512,1024]{3,2,1,0:T(8,128)(2,1)S(1)}, bf16[2,1,512,1024]{3,2,1,0:T(8,128)(2,1)}, u32[]{:S(2)}) %copy-start) | copy-done | bytes 2097176
  2.2 0.0 copy-start.1
  2.2 1.3 %copy-done.1 = bf16[16,336,128]{2,1,0:T(8,128)(2,1)S(1)} copy-done((bf16[16,336,128]{2,1,0:T(8,128)(2,1)S(1)}, bf16[16,336,128]{2,1,0:T(8,128)(2,1)}, u32[]{:S(2)}) %copy-start.1) | copy-done | bytes 1376280
  3.6 0.0 copy-start.2
  3.6 0.9 %copy-done.2 = bf16[256,256]{1,0:T(8,128)(2,1)S(1)} copy-done((bf16[256,256]{1,0:T(8,128)(2,1)S(1)}, bf16[256,256]{1,0:T(8,128)(2,1)}, u32[]{:S(2)}) %copy-start.2) | copy-done | bytes 131096
  4.5 0.0 copy-start.3
  4.5 0.9 %copy-done.3 = bf16[256,256]{1,0:T(8,128)(2,1)S(1)} copy-done((bf16[256,256]{1,0:T(8,128)(2,1)S(1)}, bf16[256,256]{1,0:T(8,128)(2,1)}, u32[]{:S(2)}) %copy-start.3) | copy-done | bytes 131096
  5.4 0.0 copy-start.4
  5.4 0.8 %copy-done.4 = bf16[256,128]{1,0:T(8,128)(2,1)S(1)} copy-done((bf16[256,128]{1,0:T(8,128)(2,1)S(1)}, bf16[256,128]{1,0:T(8,128)(2,1)}, u32[]{:S(2)}) %copy-start.4) | copy-done | bytes 65560
  6.2 0.0 copy-start.5
  6.2 0.8 %copy-done.5 = bf16[1,1,128,128]{3,2,1,0:T(8,128)(2,1)S(1)} copy-done((bf16[1,1,128,128]{3,2,1,0:T(8,128)(2,1)S(1)}, bf16[1,1,128,128]{3,2,1,0:T(8,128)(2,1)}, u32[]{:S(2)}) %copy-start.5) | copy-done | bytes 32792
  7.0 0.0 copy-start.6
  7.0 0.8 %copy-done.6 = bf16[64,256]{1,0:T(8,128)(2,1)S(1)} copy-done((bf16[64,256]{1,0:T(8,128)(2,1)S(1)}, bf16[64,256]{1,0:T(8,128)(2,1)}, u32[]{:S(2)}) %copy-start.6) | copy-done | bytes 32792
  7.7 0.0 copy-start.7
  7.7 0.7 %copy-done.7 = s32[2,2,32]{2,1,0:T(2,128)S(1)} copy-done((s32[2,2,32]{2,1,0:T(2,128)S(1)}, s32[2,2,32]{2,1,0:T(2,128)}, u32[]{:S(2)}) %copy-start.7) | copy-done | bytes 536
  8.4 38.1 %shard_map.95 = (f32[2,4,256]{2,1,0:T(4,128)S(1)}, f32[1,1,128,128]{3,2,1,0:T(8,128)S(1)}) custom-call(s32[2,2,32]{2,1,0:T(2,128)S(1)} %copy-done.7, bf16[2,1,512,1024]{3,2,1,0:T(8,128)(2,1)S(1)} %copy-done, bf16[1,1,128,128]{3,2,1,0:T(8,128)(2,1)S(1)} %copy-done.5, bf16[256,256]{1,0:T(8,128)(2,1)S(1)} %copy-done.3, bf16[256,256]{1,0:T(8,128)(2,1)S(1)} %copy-done.2, ...), custom_call_target="tpu_custom_call" | custom-call | tf_op jit(solution)/shard_map/pallas_call | solution.py:442
  46.5 0.6 %copy.12 = f32[2,4,256]{2,1,0:T(4,128)} copy(f32[2,4,256]{2,1,0:T(4,128)S(1)} %get-tuple-element.4) | data formatting | bytes 16384
  47.1 0.6 %copy.13 = f32[1,1,128,128]{3,2,1,0:T(8,128)} copy(f32[1,1,128,128]{3,2,1,0:T(8,128)S(1)} %get-tuple-element.5) | data formatting | bytes 131072
Async XLA Ops:
  0.6 1.6 %copy-start = (bf16[2,1,512,1024]{3,2,1,0:T(8,128)(2,1)S(1)}, bf16[2,1,512,1024]{3,2,1,0:T(8,128)(2,1)}, u32[]{:S(2)}) copy-start(bf16[2,1,512,1024]{3,2,1,0:T(8,128)(2,1)} %frames.1) | copy-start | bytes 6291460
  2.2 1.3 %copy-start.1 = (bf16[16,336,128]{2,1,0:T(8,128)(2,1)S(1)}, bf16[16,336,128]{2,1,0:T(8,128)(2,1)}, u32[]{:S(2)}) copy-start(bf16[16,336,128]{2,1,0:T(8,128)(2,1)} %constant.14.clone.ext_h) | copy-start | bytes 4128772
  3.6 0.9 %copy-start.2 = (bf16[256,256]{1,0:T(8,128)(2,1)S(1)}, bf16[256,256]{1,0:T(8,128)(2,1)}, u32[]{:S(2)}) copy-start(bf16[256,256]{1,0:T(8,128)(2,1)} %constant.11.clone.dc_h) | copy-start | bytes 393220
  4.5 0.9 %copy-start.3 = (bf16[256,256]{1,0:T(8,128)(2,1)S(1)}, bf16[256,256]{1,0:T(8,128)(2,1)}, u32[]{:S(2)}) copy-start(bf16[256,256]{1,0:T(8,128)(2,1)} %constant.10.clone.dr_h) | copy-start | bytes 393220
  5.4 0.8 %copy-start.4 = (bf16[256,128]{1,0:T(8,128)(2,1)S(1)}, bf16[256,128]{1,0:T(8,128)(2,1)}, u32[]{:S(2)}) copy-start(bf16[256,128]{1,0:T(8,128)(2,1)} %constant.13.clone.ex_h) | copy-start | bytes 196612
  6.2 0.8 %copy-start.5 = (bf16[1,1,128,128]{3,2,1,0:T(8,128)(2,1)S(1)}, bf16[1,1,128,128]{3,2,1,0:T(8,128)(2,1)}, u32[]{:S(2)}) copy-start(bf16[1,1,128,128]{3,2,1,0:T(8,128)(2,1)} %y_h.1) | copy-start | bytes 98308
  7.0 0.8 %copy-start.6 = (bf16[64,256]{1,0:T(8,128)(2,1)S(1)}, bf16[64,256]{1,0:T(8,128)(2,1)}, u32[]{:S(2)}) copy-start(bf16[64,256]{1,0:T(8,128)(2,1)} %constant.12.clone.ey_h) | copy-start | bytes 98308
  7.7 0.7 %copy-start.7 = (s32[2,2,32]{2,1,0:T(2,128)S(1)}, s32[2,2,32]{2,1,0:T(2,128)}, u32[]{:S(2)}) copy-start(s32[2,2,32]{2,1,0:T(2,128)} %codes.1) | copy-start | bytes 1540

commit v3 on v2

--- a/solution.py
+++ b/solution.py
@@ -157,57 +157,58 @@
     sums[pl.ds(b, 1), :] = jnp.sum(m, axis=0, keepdims=True)
 
 
-def nyquist(gbuf, r64, dc, ey, sums, mean, q64):
-    f = dot(dc, jnp.concatenate([r64[...].astype(BF), jnp.zeros((B, B), BF)], axis=0))
-    z = jnp.zeros((32, B), F32)
-    g = gbuf[:, B : B + 16, :].astype(F32)
+def nyquist(cc, gbuf, r64, dc, ey, sums, mean, q64):
+    first = pl.multiple_of(cc * 16, 16)
+    col = jnp.where(cc == 0, r64[...], pltpu.roll(r64[...], B - 16, 1))
+    f = dot(dc, jnp.concatenate([col.astype(BF), jnp.zeros((B, B), BF)], axis=0))
+    z = jnp.zeros((48, B), F32)
+    g = gbuf[pl.ds(first, 16), B : B + 16, :].astype(F32)
     gr, gi = g[:, 0, :], g[:, 1, :]
     gr = jnp.transpose(jnp.concatenate([gr, z, gr, z], axis=0))
     gi = jnp.transpose(jnp.concatenate([gi, z, gi, z], axis=0))
     re, im = cross(f[:B], f[B:], gr, gi)
     m = magnitude(re, im)
     m64 = jnp.sum(m, axis=0, keepdims=True)
-    ln = lane((NB, B))
+    ln = lane((16, B))
     half = jnp.bitwise_and(ln, 63)
-    diag = half == lax.broadcasted_iota(jnp.int32, (NB, B), 0)
-    s = sums[...] * jnp.where(half == 0, 1.0, 2.0) + jnp.where(diag, m64, 0.0)
+    diag = half == lax.broadcasted_iota(jnp.int32, (16, B), 0)
+    s = sums[pl.ds(first, 16), :] * jnp.where(half == 0, 1.0, 2.0) + jnp.where(diag, m64, 0.0)
     s0 = jnp.sum(jnp.where(ln < 64, s, 0.0), axis=1, keepdims=True)
     s1 = jnp.sum(jnp.where(ln < 64, 0.0, s), axis=1, keepdims=True)
     mm = jnp.where(ln < 64, s0, s1) * (1.0 / (B * B)) + 1e-6
-    mean[...] = mm
+    mean[pl.ds(first, 16), :] = mm
     mrow = jnp.sum(jnp.where(diag, mm, 0.0), axis=0, keepdims=True)
-    live = jnp.bitwise_and(lane((1, B)), 63) < NB
+    live = jnp.bitwise_and(lane((1, B)), 63) < 16
     inv = 1.0 / (m + jnp.where(live, mrow, 1.0))
     w = jnp.concatenate([(re * inv).astype(BF), (im * inv).astype(BF)], axis=0)
     q64[...] = dot(ey, w)[0:32]
 
 
-def back(k, zt, codes, cr, ci, mg, mean, q64, ey, ex, win, flat):
-    i = k * 8 + zt
+def back(cc, yy, zt, n, spare, codes, cr, ci, mg, mean, q64, ey, ex, win, flat):
+    i = cc * 16 + yy * 8 + zt
     b = block_of(i)
     inv = 1.0 / (mg[i] + mean[pl.ds(i, 1), :])
     w = jnp.concatenate([(cr[i] * inv).astype(BF), (ci[i] * inv).astype(BF)], axis=0)
     q = dot(ey, w)
     half = jnp.bitwise_and(lane((32, B)), 63)
-    qi = jnp.where(half == 0, pltpu.roll(q64[...], jnp.bitwise_and(B - i, B - 1), 1), q[32:64])
-    win[k] = dot(jnp.concatenate([q[0:32].astype(BF), qi.astype(BF)], axis=1), ex)
+    qi = jnp.where(half == 0, pltpu.roll(q64[...], jnp.bitwise_and(B - (yy * 8 + zt), B - 1), 1), q[32:64])
+    win[spare] = dot(jnp.concatenate([q[0:32].astype(BF), qi.astype(BF)], axis=1), ex)
     for v in range(2):
         sy = jnp.right_shift(codes[v, 0, b], 4)
         sx = jnp.right_shift(codes[v, 1, b], 4)
-        piece = win[k, pl.ds(sy + 8, 16), :]
+        piece = win[spare, pl.ds(sy + 8, 16), :]
         piece = pltpu.roll(piece, jnp.bitwise_and(B - (8 + 32 * v) - sx, B - 1), 1)
-        row = v * 4 + (k % 2) * 2 + k // 2
-        flat[pl.ds(row, 16, stride=8), :] = piece
-
-
-def flatten(flat):
+        flat[pl.ds(n * B + v * 4 + yy * 2 + cc, 16, stride=8), :] = piece
+
+
+def flatten(flat, n):
     ln = lane((8, B))
     tiles = []
     for t in range(2):
         out = None
         for k in range(8):
             a = t * 8 + k
-            piece = flat[a * 8 : a * 8 + 8, :]
+            piece = flat[pl.ds(pl.multiple_of(n * B + a * 8, 8), 8), :]
             if k:
                 piece = pltpu.roll(piece, 16 * k, 1)
             out = piece if out is None else jnp.where(ln >= 16 * k, piece, out)
@@ -216,12 +217,23 @@
 
 
 MESH = pl.DeviceIdType.MESH
-ANY = pl.BlockSpec(memory_space=pl.ANY)
+ANY = pl.BlockSpec(memory_space=pltpu.HBM)
 VM = pl.BlockSpec(memory_space=pltpu.VMEM)
 SM = pl.BlockSpec(memory_space=pltpu.SMEM)
 NEAR = (1, 7, 2, 6, 3, 5, 4)
-FAR = (4, 3, 5, 2, 6, 1, 7, 0)
-GZ, GY, GS, SA, SY, SZ, CP, NSEM = 0, 8, 16, 32, 34, 42, 50, 58
+ORDER = (4, 3, 5, 2, 6, 1, 7, 0)
+GZ, GY, GS, SA, SY, SZ, CP, NSEM = 0, 8, 16, 32, 34, 34, 42, 50
+
+
+def WARP_EVENTS(chain, z, y, send_a, await_a, zs):
+    return dict(
+        _1=send_a(0), _3=send_a(1), _5=z(1, 7), _6=chain(z(2, 6), y(0)), _7=chain(await_a(0), zs(4, 3)))
+
+
+def FRONT_EVENTS(chain, z, y, send_a, await_a, zs):
+    return dict(
+        _0=chain(z(3, 5), zs(5, 2)), _1=chain(z(4), await_a(1), zs(6, 1)), _2=chain(y(1, 7), zs(7)), _3=y(2, 6),
+        _5=y(3, 5), _7=y(4))
 
 
 def kernel(codes, frames, y_h, dr_h, dc_h, ey_h, ex_h, ext_h, out_c, out_t,
@@ -248,15 +260,15 @@
     def spectrum_copy(at_slot, sem, dev):
         return copy(g.at[at_slot], g.at[at_slot], sem, dev)
 
-    barrier = pltpu.get_barrier_semaphore()
-    greeted = up[1:] + [across, sibling] + peers[1:]
-    for dev in greeted:
-        pl.semaphore_signal(barrier, inc=1, device_id=dev, device_id_type=MESH)
     loads = [pltpu.make_async_copy(a, b, local.at[n]) for n, (a, b) in enumerate(
         ((y_h.at[0, 0], y), (dr_h, dr), (dc_h, dc), (ext_h, ext),
          (frames.at[:, 0], x.at[:, 16:528, B:1152]), (ey_h, ey), (ex_h, ex)))]
     for cp in loads:
         cp.start()
+    barrier = pltpu.get_barrier_semaphore()
+    greeted = up[1:] + [across, sibling] + peers[1:]
+    for dev in greeted:
+        pl.semaphore_signal(barrier, inc=1, device_id=dev, device_id_type=MESH)
     x[:, 0:16, :] = jnp.zeros((2, 16, 1280), BF)
     x[:, 528:544, :] = jnp.zeros((2, 16, 1280), BF)
     x[:, 16:528, 0:B] = jnp.zeros((2, 512, B), BF)
@@ -268,13 +280,13 @@
     main, nyq = own_spectrum(y[...], dr[...], dc[...])
     g[mine, 0:B, :] = main
     g[mine, B : B + 16, :] = nyq
-    loads[3].wait()
-    stage_tables(ext, extc, extr)
     pl.semaphore_wait(barrier, len(greeted))
     for d in NEAR:
         spectrum_copy(mine, GZ + d, up[d]).start()
     spectrum_copy(mine, GY, across).start()
     spectrum_copy(mine, GS, sibling).start()
+    loads[3].wait()
+    stage_tables(ext, extc, extr)
     for cp in loads[4:]:
         cp.wait()
 
@@ -297,122 +309,130 @@
     def sum_a(n):
         return copy(part.at[pl.ds(8 * n, 8)], ra.at[pl.ds(8 * n, 8)], SA + n, sibling)
 
-    def sum_y(d):
-        t = (z + d) % 8
-        return copy(sb.at[t], rb.at[t], SY + d, across)
-
     def sum_z(d):
-        return copy(sc.at[(z + d) % 8], rc.at[d - 1], SZ + d, up[d])
-
-    def both(w):
-        return part[16 + w].astype(F32) + ra[w].astype(F32)
-
-    def send_y():
-        sum_a(0).wait_recv()
-        for d in FAR:
-            t = (z + d) % 8
-            sb[t] = both(t).astype(BF)
-        for d in FAR:
-            sum_y(d).start()
+        return copy(sc.at[ORDER.index(d)], rc.at[d - 1], SZ + d, up[d])
+
+    def sum_y():
+        return copy(sb, rb, SY, across)
+
+    def pair(d):
+        n = ORDER.index(d)
+        here, there = part[16 + 2 * n : 18 + 2 * n], ra[2 * n : 2 * n + 2]
+        return here.astype(F32) + there.astype(F32)
 
     def send_z(ds):
         for d in ds:
-            sum_y(d).wait_recv()
-            t = (z + d) % 8
-            total = both(8 + t) + rb[t].astype(F32)
-            if d == 0:
-                own[...] = total
-            else:
-                sc[t] = total.astype(BF)
-                sum_z(d).start()
+            sc[ORDER.index(d)] = pair(d).astype(BF)
+            sum_z(d).start()
 
     def slot_of(w):
         cc = jnp.where(w < 16, 1 - c, c)
-        yy = jnp.where((w // 8) % 2 == 0, 1 - yh, yh)
-        return cc * 16 + yy * 8 + w % 8
-
-    def phase(step, events, order):
-        def quarter(n, _):
-            q = n if order else 3 - n
-
-            def one(j, _):
-                step(q * 8 + j)
-                return 0
-
-            lax.fori_loop(0, 8, one, 0, unroll=UN)
-            for k, event in events.items():
-                pl.when(n == k)(event)
+        m = (w % 16) // 4
+        d = jnp.where((w // 2) % 2 == 0, 4 + m, 3 - m)
+        return cc * 16 + (w % 2) * 8 + (z + d) % 8
+
+    def phase(step, order, **events):
+        def group(n, _):
+            for j in range(4):
+                step((n if order else 7 - n) * 4 + j)
+            for name, event in events.items():
+                pl.when(n == int(name[1:]))(event)
             return 0
 
-        lax.fori_loop(0, 4, quarter, 0)
+        lax.fori_loop(0, 8, group, 0)
+
+    def z_arrivals(*ds):
+        for d in ds:
+            z_arrived(d)
+
+    def y_arrivals(*ds):
+        for d in ds:
+            y_arrived(d)
 
     def warp_step(w):
         part[w] = warp_block(slot_of(w), codes, x, extc, extr).astype(BF)
 
-    def after_1():
-        sum_a(1).start()
-        z_arrived(1)
-        z_arrived(7)
-
-    def after_2():
-        send_y()
-        z_arrived(2)
-        z_arrived(6)
-
-    def after_3():
-        z_arrived(3)
-        z_arrived(5)
-
-    phase(warp_step, {0: lambda: sum_a(0).start(), 1: after_1, 2: after_2, 3: after_3}, True)
+    def z_event(*ds):
+        return lambda: z_arrivals(*ds)
+
+    def y_event(*ds):
+        return lambda: y_arrivals(*ds)
+
+    def chain(*events):
+        def run():
+            for event in events:
+                event()
+        return run
+
+    def send_a(n):
+        return lambda: sum_a(n).start()
+
+    def z_sums(*ds):
+        return lambda: send_z(ds)
+
+    def await_a(n):
+        return lambda: sum_a(n).wait_recv()
+
+    phase(warp_step, True, **WARP_EVENTS(chain, z_event, y_event, send_a, await_a, z_sums))
 
     def front_step(w):
         front(slot_of(w), x, dr[...], dc[...], r64, cr, ci)
 
-    def front_0():
-        z_arrived(4)
-        y_arrived(0)
-
-    def arrivals(*ds):
-        def event():
-            for d in ds:
-                y_arrived(d)
-        return event
-
-    phase(front_step, {0: front_0, 1: arrivals(1, 7), 2: arrivals(2, 6), 3: arrivals(3, 5, 4)}, True)
-
-    def middle_step(w):
-        middle(slot_of(w), g, cr, ci, mg, sums)
-
-    def middle_0():
-        sum_a(1).wait_recv()
-        send_z(FAR[:4])
-
-    def middle_1():
-        send_z(FAR[4:])
-        sibling_arrived(0)
-
-    phase(middle_step, {0: middle_0, 1: middle_1, 2: lambda: sibling_arrived(1)}, False)
-    nyquist(g, r64, dc[...], ey[...], sums, mean, q64)
+    phase(front_step, True, **FRONT_EVENTS(chain, z_event, y_event, send_a, await_a, z_sums))
 
     def window_copy(d):
         return copy(sent.at[d], rp.at[d - 1], CP + d, peers[d])
 
-    def back_step(n, _):
-        zt = (p + 1 + n) % 8
-        for k in range(4):
-            back(k, zt, codes, cr, ci, mg, mean, q64, ey[...], ex[...], win, flat)
-        sent[(n + 1) % 8] = flatten(flat)
-        for d in range(1, 8):
-            pl.when(n == d - 1)(lambda d=d: window_copy(d).start())
-        return 0
-
-    lax.fori_loop(0, 8, back_step, 0)
+    def correlate(cc, last):
+        def middle_group(n, _):
+            if last:
+                pl.when(n == 0)(lambda: sibling_arrived(0))
+                pl.when(n == 2)(lambda: sibling_arrived(1))
+            for j in range(4):
+                middle(slot(cc, jnp.where(n < 2, yh, 1 - yh), (n % 2) * 4 + j), g, cr, ci, mg, sums)
+            return 0
+
+        lax.fori_loop(0, 4, middle_group, 0)
+        nyquist(cc, g, r64, dc[...], ey[...], sums, mean, q64)
+
+        def back_pair(h, _):
+            for e in range(2):
+                n = 2 * h + e
+                zt = (p + 1 + n) % 8
+                for yy in range(2):
+                    back(cc, yy, zt, n, 2 * e + yy, codes, cr, ci, mg, mean, q64, ey[...], ex[...], win, flat)
+                if last:
+                    sent[(n + 1) % 8] = flatten(flat, n)
+            if last:
+                for d in range(1, 8):
+                    pl.when(h == (d - 1) // 2)(lambda d=d: window_copy(d).start())
+            return 0
+
+        lax.fori_loop(0, 4, back_pair, 0)
+
+    correlate(c, False)
+    correlate(1 - c, True)
     for d in range(1, 8):
         sum_z(d).wait_recv()
-    total = own[...]
-    for d in range(7):
-        total = total + rc[d].astype(F32)
-    out_t[0, 0] = total * (1.0 / 64)
+
+    def summed(yy):
+        total = part[30 + yy].astype(F32) + ra[14 + yy].astype(F32)
+        for d in range(7):
+            total = total + rc[d, yy].astype(F32)
+        return total
+
+    sb[...] = summed(1 - yh).astype(BF)
+    sum_y().start()
+    own[...] = summed(yh)
+    for d in range(8):
+        if d:
+            spectrum_copy(mine, GZ + d, up[d]).wait_send()
+            sum_z(d).wait_send()
+        spectrum_copy(mine, GY + d, across).wait_send()
+        spectrum_copy(mine, GS + d, sibling).wait_send()
+        spectrum_copy(mine, GS + 8 + d, sibling).wait_send()
+    sum_a(0).wait_send()
+    sum_a(1).wait_send()
     for d in range(1, 8):
         window_copy(d).wait_recv()
     total = sent[0]
@@ -420,20 +440,11 @@
         total = total + rp[d]
     out_c[0] = total[0:4]
     out_c[1] = total[4:8]
+    sum_y().wait_recv()
+    out_t[0, 0] = (own[...] + rb[...].astype(F32)) * (1.0 / 64)
+    sum_y().wait_send()
     for d in range(1, 8):
-        spectrum_copy(mine, GZ + d, up[d]).wait_send()
-        sum_z(d).wait_send()
         window_copy(d).wait_send()
-    for d in range(8):
-        spectrum_copy(mine, GY + d, across).wait_send()
-        spectrum_copy(mine, GS + d, sibling).wait_send()
-        spectrum_copy(mine, GS + 8 + d, sibling).wait_send()
-        sum_y(d).wait_send()
-    sum_a(0).wait_send()
-    sum_a(1).wait_send()
-
-
-UN = 4
 
 
 def on_device(frames, template, codes):
@@ -450,13 +461,13 @@
             vm((NB, 144, B), BF), vm((B, B), F32),
             vm((NB, B, B), F32), vm((NB, B, B), F32), vm((NB, B, B), F32),
             vm((NB, B), F32), vm((NB, B), F32), vm((32, B), F32),
-            vm((4, 32, B), F32), vm((B, B), F32), vm((8, 8, 2 * B), F32),
-            vm((NB, B, B), BF), vm((16, B, B), BF), vm((8, B, B), BF), vm((8, B, B), BF),
-            vm((8, B, B), BF), vm((7, B, B), BF), vm((7, 8, 2 * B), F32), vm((B, B), F32),
+            vm((4, 32, B), F32), vm((8 * B, B), F32), vm((8, 8, 2 * B), F32),
+            vm((NB, B, B), BF), vm((16, B, B), BF), vm((B, B), BF), vm((B, B), BF),
+            vm((8, 2, B, B), BF), vm((7, 2, B, B), BF), vm((7, 8, 2 * B), F32), vm((B, B), F32),
             dma((7,)), dma((NSEM,)), dma((NSEM,)),
         ],
         compiler_params=pltpu.CompilerParams(
-            collective_id=0, has_side_effects=True, vmem_limit_bytes=48 * 2**20),
+            collective_id=0, has_side_effects=True, vmem_limit_bytes=67043328),
     )(codes, frames, template, *tables())
 
 

time: 48.1 us -> 40.6 us (0.84)
  local copies, waits for them, and re-layouts: 8.99 us -> 2.77 us
  Pallas kernels: 38.1 us -> 36.8 us
    unnamed x18 -> x2, local copies, waits for them, and re-layouts: 8.99 us -> 2.77 us
    pallas_call x1, Pallas kernels: 38.1 us -> 36.8 us  [on_device(): pl.pallas_call(kernel, out_shape=[jax.ShapeDtypeStruct((2, 4, 256), F32),...]
where the time goes in v3:
time: 40.6 us; the launch traced here: 40.2 us
  Pallas kernels  36.8 us (91%)
  local copies, waits for them, and re-layouts  2.77 us (7%)
  between operations  0.64 us (2%)
    pallas_call x1, Pallas kernels, on_device(): pl.pallas_call(kernel, out_shape=[jax.ShapeDtypeStruct((2, 4, 256), F32),...  36.8 us
    unnamed x2, local copies, waits for them, and re-layouts  2.77 us

profile of v3, /device:TPU:8, one launch (start us, length us, event | category | flops | bytes accessed | tf_op | source)
XLA Modules:
  0.0 40.2 jit_solution(13967617509667457471)
XLA Ops:
  0.6 36.8 %shard_map.95 = (f32[2,4,256]{2,1,0:T(4,128)}, f32[1,1,128,128]{3,2,1,0:T(8,128)}) custom-call(s32[2,2,32]{2,1,0:T(2,128)} %codes.1, bf16[2,1,512,1024]{3,2,1,0:T(8,128)(2,1)} %frames.1, bf16[1,1,128,128]{3,2,1,0:T(8,128)(2,1)} %y_h.1, bf16[256,256]{1,0:T(8,128)(2,1)} %constant.10.clone.dr_h, bf16[256,256]{1,0:T(8,128)(2,1)} %constant.11.clone.dc_h, ...), custom_call_target="tpu_custom_call" | custom-call | tf_op jit(solution)/shard_map/pallas_call | solution.py:453
  37.4 1.3 %copy.12 = f32[2,4,256]{2,1,0:T(4,128)} copy(f32[2,4,256]{2,1,0:T(4,128)} %get-tuple-element.4) | data formatting | bytes 16384
  38.7 1.5 %copy.13 = f32[1,1,128,128]{3,2,1,0:T(8,128)} copy(f32[1,1,128,128]{3,2,1,0:T(8,128)} %get-tuple-element.5) | data formatting | bytes 131072

commit v4 on v3

--- a/solution.py
+++ b/solution.py
@@ -226,14 +226,11 @@
 
 
 def WARP_EVENTS(chain, z, y, send_a, await_a, zs):
-    return dict(
-        _1=send_a(0), _3=send_a(1), _5=z(1, 7), _6=chain(z(2, 6), y(0)), _7=chain(await_a(0), zs(4, 3)))
+    return dict(_1=send_a(0), _3=send_a(1), _5=chain(await_a(0), zs(4, 3)), _6=chain(z(1, 7), y(0), zs(5, 2)), _7=chain(z(2, 6), await_a(1), zs(6, 1)))
 
 
 def FRONT_EVENTS(chain, z, y, send_a, await_a, zs):
-    return dict(
-        _0=chain(z(3, 5), zs(5, 2)), _1=chain(z(4), await_a(1), zs(6, 1)), _2=chain(y(1, 7), zs(7)), _3=y(2, 6),
-        _5=y(3, 5), _7=y(4))
+    return dict(_0=zs(7), _1=z(3, 5), _2=z(4), _3=y(1, 7), _4=y(2, 6), _6=y(3, 5), _7=y(4))
 
 
 def kernel(codes, frames, y_h, dr_h, dc_h, ey_h, ex_h, ext_h, out_c, out_t,
@@ -395,9 +392,9 @@
         lax.fori_loop(0, 4, middle_group, 0)
         nyquist(cc, g, r64, dc[...], ey[...], sums, mean, q64)
 
-        def back_pair(h, _):
-            for e in range(2):
-                n = 2 * h + e
+        def back_groups(h, _):
+            for e in range(4):
+                n = 4 * h + e
                 zt = (p + 1 + n) % 8
                 for yy in range(2):
                     back(cc, yy, zt, n, 2 * e + yy, codes, cr, ci, mg, mean, q64, ey[...], ex[...], win, flat)
@@ -405,10 +402,10 @@
                     sent[(n + 1) % 8] = flatten(flat, n)
             if last:
                 for d in range(1, 8):
-                    pl.when(h == (d - 1) // 2)(lambda d=d: window_copy(d).start())
+                    pl.when(h == (d - 1) // 4)(lambda d=d: window_copy(d).start())
             return 0
 
-        lax.fori_loop(0, 4, back_pair, 0)
+        lax.fori_loop(0, 2, back_groups, 0)
 
     correlate(c, False)
     correlate(1 - c, True)
@@ -461,7 +458,7 @@
             vm((NB, 144, B), BF), vm((B, B), F32),
             vm((NB, B, B), F32), vm((NB, B, B), F32), vm((NB, B, B), F32),
             vm((NB, B), F32), vm((NB, B), F32), vm((32, B), F32),
-            vm((4, 32, B), F32), vm((8 * B, B), F32), vm((8, 8, 2 * B), F32),
+            vm((8, 32, B), F32), vm((8 * B, B), F32), vm((8, 8, 2 * B), F32),
             vm((NB, B, B), BF), vm((16, B, B), BF), vm((B, B), BF), vm((B, B), BF),
             vm((8, 2, B, B), BF), vm((7, 2, B, B), BF), vm((7, 8, 2 * B), F32), vm((B, B), F32),
             dma((7,)), dma((NSEM,)), dma((NSEM,)),

time: 40.6 us -> 39.6 us (0.975)
  Pallas kernels: 36.8 us -> 36 us
    pallas_call x1, Pallas kernels: 36.8 us -> 36 us  [on_device(): pl.pallas_call(kernel, out_shape=[jax.ShapeDtypeStruct((2, 4, 256), F32),...]
where the time goes in v4:
time: 39.6 us; the launch traced here: 39.4 us
  Pallas kernels  36 us (91%)
  local copies, waits for them, and re-layouts  2.77 us (7%)
  between operations  0.64 us (2%)
    pallas_call x1, Pallas kernels, on_device(): pl.pallas_call(kernel, out_shape=[jax.ShapeDtypeStruct((2, 4, 256), F32),...  36 us
    unnamed x2, local copies, waits for them, and re-layouts  2.77 us

profile of v4, /device:TPU:8, one launch (start us, length us, event | category | flops | bytes accessed | tf_op | source)
XLA Modules:
  0.0 39.4 jit_solution(10307768960329943246)
XLA Ops:
  0.6 36.0 %shard_map.95 = (f32[2,4,256]{2,1,0:T(4,128)}, f32[1,1,128,128]{3,2,1,0:T(8,128)}) custom-call(s32[2,2,32]{2,1,0:T(2,128)} %codes.1, bf16[2,1,512,1024]{3,2,1,0:T(8,128)(2,1)} %frames.1, bf16[1,1,128,128]{3,2,1,0:T(8,128)(2,1)} %y_h.1, bf16[256,256]{1,0:T(8,128)(2,1)} %constant.10.clone.dr_h, bf16[256,256]{1,0:T(8,128)(2,1)} %constant.11.clone.dc_h, ...), custom_call_target="tpu_custom_call" | custom-call | tf_op jit(solution)/shard_map/pallas_call | solution.py:450
  36.6 1.3 %copy.12 = f32[2,4,256]{2,1,0:T(4,128)} copy(f32[2,4,256]{2,1,0:T(4,128)} %get-tuple-element.4) | data formatting | bytes 16384
  37.9 1.5 %copy.13 = f32[1,1,128,128]{3,2,1,0:T(8,128)} copy(f32[1,1,128,128]{3,2,1,0:T(8,128)} %get-tuple-element.5) | data formatting | bytes 131072

commit v5 on v4

--- a/solution.py
+++ b/solution.py
@@ -257,15 +257,15 @@
     def spectrum_copy(at_slot, sem, dev):
         return copy(g.at[at_slot], g.at[at_slot], sem, dev)
 
+    barrier = pltpu.get_barrier_semaphore()
+    greeted = [up[d] for d in ORDER[:-1]] + peers[1:] + [across, sibling]
+    for dev in greeted:
+        pl.semaphore_signal(barrier, inc=1, device_id=dev, device_id_type=MESH)
     loads = [pltpu.make_async_copy(a, b, local.at[n]) for n, (a, b) in enumerate(
         ((y_h.at[0, 0], y), (dr_h, dr), (dc_h, dc), (ext_h, ext),
          (frames.at[:, 0], x.at[:, 16:528, B:1152]), (ey_h, ey), (ex_h, ex)))]
     for cp in loads:
         cp.start()
-    barrier = pltpu.get_barrier_semaphore()
-    greeted = up[1:] + [across, sibling] + peers[1:]
-    for dev in greeted:
-        pl.semaphore_signal(barrier, inc=1, device_id=dev, device_id_type=MESH)
     x[:, 0:16, :] = jnp.zeros((2, 16, 1280), BF)
     x[:, 528:544, :] = jnp.zeros((2, 16, 1280), BF)
     x[:, 16:528, 0:B] = jnp.zeros((2, 512, B), BF)

time: 39.6 us -> 39.5 us (level)
  no operation moved by 1% of the time
where the time goes in v5:
time: 39.5 us; the launch traced here: 39.3 us
  Pallas kernels  35.9 us (91%)
  local copies, waits for them, and re-layouts  2.77 us (7%)
  between operations  0.64 us (2%)
    pallas_call x1, Pallas kernels, on_device(): pl.pallas_call(kernel, out_shape=[jax.ShapeDtypeStruct((2, 4, 256), F32),...  35.9 us
    unnamed x2, local copies, waits for them, and re-layouts  2.77 us

profile of v5, /device:TPU:8, one launch (start us, length us, event | category | flops | bytes accessed | tf_op | source)
XLA Modules:
  0.0 39.3 jit_solution(15672123094606772151)
XLA Ops:
  0.6 35.9 %shard_map.95 = (f32[2,4,256]{2,1,0:T(4,128)}, f32[1,1,128,128]{3,2,1,0:T(8,128)}) custom-call(s32[2,2,32]{2,1,0:T(2,128)} %codes.1, bf16[2,1,512,1024]{3,2,1,0:T(8,128)(2,1)} %frames.1, bf16[1,1,128,128]{3,2,1,0:T(8,128)(2,1)} %y_h.1, bf16[256,256]{1,0:T(8,128)(2,1)} %constant.10.clone.dr_h, bf16[256,256]{1,0:T(8,128)(2,1)} %constant.11.clone.dc_h, ...), custom_call_target="tpu_custom_call" | custom-call | tf_op jit(solution)/shard_map/pallas_call | solution.py:450
  36.6 1.3 %copy.12 = f32[2,4,256]{2,1,0:T(4,128)} copy(f32[2,4,256]{2,1,0:T(4,128)} %get-tuple-element.4) | data formatting | bytes 16384
  37.9 1.5 %copy.13 = f32[1,1,128,128]{3,2,1,0:T(8,128)} copy(f32[1,1,128,128]{3,2,1,0:T(8,128)} %get-tuple-element.5) | data formatting | bytes 131072
